TPU v7x, 128 devices: a whole 4x4x4 slice. The times are simulated.
128 devices in a mesh: ty: 4 (over y), tx: 32 (over x, z, core).
Axes of the slice: x: 4, y: 4, z: 4, core: 2. Of those that a mesh axis runs over, the one named last changes fastest.
Arguments:
- velocity_start: float32 [2, 10, 128, 8192], P(None, None, 'ty', 'tx'), may hold values from -4 to 4
- stiffness: float32 [10, 128, 8192], P(None, 'ty', 'tx'), may hold values from 0.3 to 3
- beta: float32 [128, 8192], P('ty', 'tx'), may hold values from 0.1 to 10
- ice_mask: int32 [128, 8192], P('ty', 'tx'), may hold values 0 or 1
- thickness: float32 [128, 8192], P('ty', 'tx'), may hold values from 0.5 to 2
- bed: float32 [128, 8192], P('ty', 'tx'), may hold values from -18 to 18
- land_smb: float32 [10, 65536], P(None, ('ty', 'tx')), may hold values from -6 to 6
- elev_class: int32 [128, 8192], P('ty', 'tx'), may hold values from 0 to 9
- correlation_cols: int32 [4, 128, 8192], P(None, 'ty', 'tx'), may hold values from 0 to 65535
- correlation_weights: float32 [4, 128, 8192], P(None, 'ty', 'tx'), may hold values from 0.1 to 1
Outputs:
- velocity: float32 [2, 10, 128, 8192], P(None, None, 'ty', 'tx')
- surface: float32 [128, 8192], P('ty', 'tx')
- land_surface: float32 [10, 65536], P(None, ('ty', 'tx'))
All inputs are finite; a program needn't handle non-finite values. No bound on the sum of `ice_mask` on one device may be relied on, other than what follows from the above.
Results may differ from a plain program's by a relative error of at most 0.0001.
Values sent between devices are 32-bit elements; how exact they have to be, the bound alone decides.
A program may use at most 64 MiB of HBM per device.

v0:
```python
import functools
import jax
import jax.numpy as jnp
from jax import lax
from jax.experimental import pallas as pl
from jax.experimental.pallas import tpu as pltpu
from jax.sharding import PartitionSpec as P

MESH = pl.DeviceIdType.MESH
F32 = jnp.float32
BF = jnp.bfloat16
VM = pl.BlockSpec(memory_space=pltpu.VMEM)
SM = pl.BlockSpec(memory_space=pltpu.SMEM)
SLOTS = 128
HIGH = 64
NT = (((1,), (1,)), ((), ()))


def parts(x, count):
    out = []
    for _ in range(count):
        top = x.astype(BF)
        out.append(top)
        x = x - top.astype(F32)
    return out


def is_row(size, row):
    return lax.broadcasted_iota(jnp.int32, (size, row.shape[1]), 0) == row


def hot(size, row):
    return jnp.where(is_row(size, row), 1.0, 0.0).astype(BF)


def route_kernel(peers, turn_ref, cols_ref, class_ref, weights_ref, send_ref, cell_ref, most_ref, left_ref, right_ref, total_ref):
    width = cols_ref.shape[1]
    step = 8
    before = lax.broadcasted_iota(jnp.int32, (width, 2 * width), 0) < lax.broadcasted_iota(
        jnp.int32, (width, 2 * width), 1
    )
    ahead = jnp.where(before, 1.0, 0.0).astype(BF)
    first = turn_ref[0] * SLOTS
    most = jnp.zeros((peers, width), F32)
    for k in range(4):
        total_ref[...] = jnp.zeros_like(total_ref)

        def body(g, base):
            at = pl.multiple_of(k * 32 + g * step, step)
            cols = cols_ref[pl.ds(at, step), :]
            kind = class_ref[pl.ds(pl.multiple_of(g * step, step), step), :]
            dest = cols >> 9
            lane = lax.broadcasted_iota(jnp.int32, cols.shape, 1)
            row = lax.broadcasted_iota(jnp.int32, cols.shape, 0) + g * step
            whole = (kind * 4 + ((cols >> 7) & 3), cols & 127, row * 2 + (lane >> 7), lane & 127)
            fields = [v.astype(F32) for v in whole]
            w = weights_ref[pl.ds(at, step), :]
            w_top = w.astype(BF).astype(F32)
            fields += [w_top, w - w_top]
            for r in range(step):
                one = slice(r, r + 1)
                mask = is_row(peers, dest[one])
                picked = jnp.where(mask, 1.0, 0.0).astype(BF)
                counts = jnp.dot(picked, ahead, preferred_element_type=F32)
                rank = jnp.sum(jnp.where(mask, counts[:, :width] + base, 0.0), axis=0, keepdims=True)
                base = base + counts[:, width:]
                span = pl.ds(r * width, width)
                for f, value in enumerate(fields):
                    left_ref[f * peers : (f + 1) * peers, span] = picked * value[one].astype(BF)
                right_ref[:, span] = hot(SLOTS, rank.astype(jnp.int32) - first)
            total_ref[...] += lax.dot_general(left_ref[...], right_ref[...], NT, preferred_element_type=F32)
            return base

        base = lax.fori_loop(0, 32 // step, body, jnp.zeros((peers, width), F32))
        f = [total_ref[i * peers : (i + 1) * peers, :] for i in range(6)]
        send_ref[:, k, :] = f[0] * 128.0 + f[1]
        cell_ref[:, k, :] = f[2] * 128.0 + f[3]
        send_ref[:, 4 + k, :] = f[4] + f[5]
        most = jnp.maximum(most, base)
    most_ref[...] = jnp.broadcast_to(jnp.max(most, keepdims=True), most_ref.shape)


def route(turn, cols, kind, weights, peers=128):
    rows, width = 4 * cols.shape[1], cols.shape[2]
    return pl.pallas_call(
        functools.partial(route_kernel, peers),
        name="route",
        out_shape=(
            jax.ShapeDtypeStruct((peers, 8, SLOTS), F32),
            jax.ShapeDtypeStruct((peers, 4, SLOTS), F32),
            jax.ShapeDtypeStruct((8, 128), F32),
        ),
        in_specs=[SM, VM, VM, VM],
        out_specs=(VM, VM, VM),
        scratch_shapes=[
            pltpu.VMEM((6 * peers, 8 * width), BF),
            pltpu.VMEM((SLOTS, 8 * width), BF),
            pltpu.VMEM((6 * peers, SLOTS), F32),
        ],
        compiler_params=pltpu.CompilerParams(vmem_limit_bytes=48 << 20),
    )(turn, cols.reshape(rows, width), kind, weights.reshape(rows, width))


def spots(where):
    at = where.astype(jnp.int32)
    return at >> 7, at & 127


def table_terms(table):
    padded = jnp.concatenate([table, jnp.zeros((HIGH - table.shape[0], 128), F32)], axis=0) if table.shape[0] < HIGH else table
    return jnp.concatenate([p.astype(F32) for p in parts(padded, 3)], axis=0).T.astype(BF)


def look_up(terms, high, low_masks):
    stacked = jnp.concatenate([high] * 3, axis=0)
    found = jnp.dot(terms, stacked, preferred_element_type=F32)
    return jnp.sum(jnp.where(low_masks, found, 0.0), axis=0, keepdims=True)


def across(pieces):
    return jnp.concatenate(pieces, axis=1)


def add_in(total_ref, values, high, low):
    both = jnp.concatenate([high * v.astype(BF) for v in values], axis=0)
    total_ref[...] += lax.dot_general(both, low, NT, preferred_element_type=F32)


GROUP = 4


def flat_rows(tiles):
    return [tiles[s, k : k + 1, :] for s in range(tiles.shape[0]) for k in range(4)]


def owner_kernel(table_ref, got_ref, denom_ref, back_ref, terms_ref, total_ref):
    terms_ref[...] = table_terms(table_ref[...])
    total_ref[...] = jnp.zeros_like(total_ref)

    @pl.loop(0, got_ref.shape[0] // GROUP)
    def _(g):
        tile = got_ref[pl.ds(g * GROUP, GROUP), :, :]
        high, low = spots(tile[:, :4, :])
        w = across(flat_rows(tile[:, 4:, :]))
        high_hot = hot(HIGH, across(flat_rows(high)))
        low_mask = is_row(128, across(flat_rows(low)))
        low_hot = jnp.where(low_mask, 1.0, 0.0).astype(BF)
        w_top = w.astype(BF).astype(F32)
        add_in(total_ref, (w_top, w - w_top), high_hot, low_hot)
        found = look_up(terms_ref[...], high_hot, low_mask)
        for s in range(GROUP):
            for k in range(4):
                i = s * 4 + k
                back_ref[g * GROUP + s, k : k + 1, :] = found[:, i * 128 : (i + 1) * 128]

    denom_ref[...] = total_ref[:HIGH, :] + total_ref[HIGH:, :]


def owner(table, got):
    peers = got.shape[0]
    return pl.pallas_call(
        owner_kernel,
        name="owner",
        out_shape=(jax.ShapeDtypeStruct((HIGH, 128), F32), jax.ShapeDtypeStruct((peers, 4, SLOTS), F32)),
        in_specs=[VM, VM],
        out_specs=(VM, VM),
        scratch_shapes=[pltpu.VMEM((128, 3 * HIGH), BF), pltpu.VMEM((2 * HIGH, 128), F32)],
        compiler_params=pltpu.CompilerParams(vmem_limit_bytes=48 << 20),
    )(table, got)


def gather_kernel(table_ref, where_ref, out_ref, terms_ref):
    terms_ref[...] = table_terms(table_ref[...])

    @pl.loop(0, where_ref.shape[0] // GROUP)
    def _(g):
        high, low = spots(where_ref[pl.ds(g * GROUP, GROUP), :, :])
        found = look_up(
            terms_ref[...], hot(HIGH, across(flat_rows(high))), is_row(128, across(flat_rows(low)))
        )
        for s in range(GROUP):
            for k in range(4):
                i = s * 4 + k
                out_ref[g * GROUP + s, k : k + 1, :] = found[:, i * 128 : (i + 1) * 128]


def gather(table, where):
    return pl.pallas_call(
        gather_kernel,
        name="pick",
        out_shape=jax.ShapeDtypeStruct(where.shape, F32),
        in_specs=[VM, VM],
        out_specs=VM,
        scratch_shapes=[pltpu.VMEM((128, 3 * HIGH), BF)],
        compiler_params=pltpu.CompilerParams(vmem_limit_bytes=48 << 20),
    )(table, where)


def scatter_kernel(first, where_ref, weights_ref, values_ref, out_ref, total_ref):
    total_ref[...] = jnp.zeros_like(total_ref)

    @pl.loop(0, where_ref.shape[0] // GROUP)
    def _(g):
        span = pl.ds(g * GROUP, GROUP)
        high, low = spots(where_ref[span, :4, :])
        v = across(flat_rows(weights_ref[span, 4:, :] * values_ref[span, :, :]))
        v_top = v.astype(BF).astype(F32)
        add_in(
            total_ref,
            (v_top, v - v_top),
            hot(HIGH, across(flat_rows(high))),
            hot(128, across(flat_rows(low))),
        )

    out_ref[...] = total_ref[:HIGH, :] + total_ref[HIGH:, :]


def scatter(where, weights, values):
    return pl.pallas_call(
        functools.partial(scatter_kernel, 0),
        name="put",
        out_shape=jax.ShapeDtypeStruct((HIGH, 128), F32),
        in_specs=[VM, VM, VM],
        out_specs=VM,
        scratch_shapes=[pltpu.VMEM((2 * HIGH, 128), F32)],
        compiler_params=pltpu.CompilerParams(vmem_limit_bytes=48 << 20),
    )(where, weights, values)


def place():
    wide = lax.axis_size("tx")
    return lax.axis_index("ty") * wide + lax.axis_index("tx"), lax.axis_size("ty") * wide


def at(peer):
    wide = lax.axis_size("tx")
    return (peer // wide, peer % wide)


def meet(me, peers):
    barrier = pltpu.get_barrier_semaphore()

    @pl.loop(1, peers)
    def _(step):
        pl.semaphore_signal(barrier, inc=1, device_id=at((me + step) % peers), device_id_type=MESH)

    pl.semaphore_wait(barrier, peers - 1)


def exchange_kernel(send_ref, got_ref, out_sem, in_sem, own_sem):
    me, peers = place()
    own = pltpu.make_async_copy(send_ref.at[me], got_ref.at[me], own_sem)
    own.start()
    meet(me, peers)

    @pl.loop(1, peers)
    def _(step):
        peer = (me + step) % peers
        pltpu.make_async_remote_copy(
            send_ref.at[peer], got_ref.at[me], out_sem, in_sem, device_id=at(peer), device_id_type=MESH
        ).start()

    own.wait()
    others = pl.ds(0, peers - 1)
    whole = pltpu.make_async_remote_copy(
        send_ref.at[others], got_ref.at[others], out_sem, in_sem, device_id=at((me + 1) % peers), device_id_type=MESH
    )
    whole.wait()


def exchange(send, name, number):
    return pl.pallas_call(
        exchange_kernel,
        name=name,
        out_shape=jax.ShapeDtypeStruct(send.shape, send.dtype),
        in_specs=[VM],
        out_specs=VM,
        scratch_shapes=[pltpu.SemaphoreType.DMA] * 3,
        compiler_params=pltpu.CompilerParams(collective_id=number, has_side_effects=True),
    )(send)


def joined(tiles):
    row = lax.broadcasted_iota(jnp.int32, tiles.shape[1:], 0)
    return jnp.where(row < 7, jnp.sum(tiles, axis=0), jnp.max(tiles, axis=0))


def total_kernel(part_ref, sum_ref, near_ref, half_ref, far_ref, near_out, near_in, far_out, far_in):
    y, x = lax.axis_index("ty"), lax.axis_index("tx")
    tall, wide = lax.axis_size("ty"), lax.axis_size("tx")
    core, chip = x % 2, x // 2
    near, far = tall * 2, wide // 2
    me = y * 2 + core
    near_ids = [(me + i) % near for i in range(1, near)]
    near_devices = [(i // 2, chip * 2 + i % 2) for i in near_ids]
    far_devices = [(y, ((chip + i) % far) * 2 + core) for i in range(1, far)]
    barrier = pltpu.get_barrier_semaphore()
    for device in near_devices + far_devices:
        pl.semaphore_signal(barrier, inc=1, device_id=device, device_id_type=MESH)
    pl.semaphore_wait(barrier, near + far - 2)
    for device in near_devices:
        pltpu.make_async_remote_copy(
            part_ref, near_ref.at[me], near_out, near_in, device_id=device, device_id_type=MESH
        ).start()
    near_ref[pl.ds(me, 1)] = part_ref[...][None]
    whole = pl.ds(0, near - 1)
    pltpu.make_async_remote_copy(
        near_ref.at[whole], near_ref.at[whole], near_out, near_in, device_id=near_devices[0], device_id_type=MESH
    ).wait()
    half = joined(near_ref[...])
    half_ref[...] = half
    for device in far_devices:
        pltpu.make_async_remote_copy(
            half_ref, far_ref.at[chip], far_out, far_in, device_id=device, device_id_type=MESH
        ).start()
    far_ref[pl.ds(chip, 1)] = half[None]
    whole = pl.ds(0, far - 1)
    pltpu.make_async_remote_copy(
        far_ref.at[whole], far_ref.at[whole], far_out, far_in, device_id=far_devices[0], device_id_type=MESH
    ).wait()
    sum_ref[...] = joined(far_ref[...])


def total(part, name, number):
    tall, wide = lax.axis_size("ty"), lax.axis_size("tx")
    shape = part.shape
    return pl.pallas_call(
        total_kernel,
        name=name,
        out_shape=jax.ShapeDtypeStruct(shape, part.dtype),
        in_specs=[VM],
        out_specs=VM,
        scratch_shapes=[
            pltpu.VMEM((tall * 2, *shape), part.dtype),
            pltpu.VMEM(shape, part.dtype),
            pltpu.VMEM((wide // 2, *shape), part.dtype),
        ]
        + [pltpu.SemaphoreType.DMA] * 4,
        compiler_params=pltpu.CompilerParams(collective_id=number, has_side_effects=True),
    )(part)


LEV = 10
ROWS, COLS = 32, 256
TALL, LONG = 48, 384
RIM = 8
PLANES = 3 * LEV + 4
MASK, THICK, BED, BETA = range(3 * LEV, PLANES)
PACKS = 3
ALL_ROWS = pl.ds(0, ROWS)


def halo_kernel(vel_ref, stiff_ref, mask_ref, thick_ref, bed_ref, beta_ref, out_ref, left_ref, right_ref, from_right, from_left, out_sem, in_sem):
    y, x = lax.axis_index("ty"), lax.axis_index("tx")
    tall, wide = lax.axis_size("ty"), lax.axis_size("tx")
    lane = lax.broadcasted_iota(jnp.int32, (ROWS, 128), 1)
    left = [jnp.zeros((ROWS, 128), F32)] * PACKS
    right = [jnp.zeros((ROWS, 128), F32)] * PACKS
    for p in range(PLANES):
        if p < 2 * LEV:
            plane = vel_ref[p]
        elif p < 3 * LEV:
            plane = stiff_ref[p - 2 * LEV]
        elif p == MASK:
            plane = mask_ref[...].astype(F32)
        else:
            plane = {THICK: thick_ref, BED: bed_ref, BETA: beta_ref}[p][...]
        out_ref[p, :ROWS, :COLS] = plane
        pack, k = p // 16, p % 16
        here = (lane >= RIM * k) & (lane < RIM * (k + 1))
        first, last = plane[:, :128], plane[:, COLS - 128 :]
        left[pack] = jnp.where(here, pltpu.roll(first, RIM * k, 1) if k else first, left[pack])
        turn = (RIM * k + RIM) % 128
        right[pack] = jnp.where(here, pltpu.roll(last, turn, 1) if turn else last, right[pack])
    for i in range(PACKS):
        left_ref[i] = left[i]
        right_ref[i] = right[i]
    around = [(a, b) for a in (-1, 0, 1) for b in (-1, 0, 1) if (a, b) != (0, 0)]
    where = [((y + a + tall) % tall, (x + b + wide) % wide) for a, b in around]
    barrier = pltpu.get_barrier_semaphore()
    for device in where:
        pl.semaphore_signal(barrier, inc=1, device_id=device, device_id_type=MESH)
    pl.semaphore_wait(barrier, len(where))
    copies = []
    for i, ((a, b), device) in enumerate(zip(around, where)):
        rows = {-1: pl.ds(0, RIM), 0: ALL_ROWS, 1: pl.ds(ROWS - RIM, RIM)}[a]
        there = {-1: pl.ds(ROWS, RIM), 0: ALL_ROWS, 1: pl.ds(TALL - RIM, RIM)}[a]
        if b == 0:
            ends = out_ref.at[:, rows, pl.ds(0, COLS)], out_ref.at[:, there, pl.ds(0, COLS)]
        elif b < 0:
            ends = left_ref.at[:, rows, :], from_right.at[:, there, :]
        else:
            ends = right_ref.at[:, rows, :], from_left.at[:, there, :]
        copies.append(
            pltpu.make_async_remote_copy(
                *ends, out_sem.at[i], in_sem.at[i], device_id=device, device_id_type=MESH
            )
        )
        copies[-1].start()
    for copy in copies:
        copy.wait()
    row = lax.broadcasted_iota(jnp.int32, (TALL, 128), 0)
    lane = lax.broadcasted_iota(jnp.int32, (TALL, 128), 1)
    inside = (row < ROWS) | ((row < ROWS + RIM) & (y < tall - 1)) | ((row >= TALL - RIM) & (y > 0))
    on_right = inside & (lane < RIM) & (x < wide - 1)
    on_left = inside & (lane >= 128 - RIM) & (x > 0)
    rights = [from_right[i] for i in range(PACKS)]
    lefts = [from_left[i] for i in range(PACKS)]
    for p in range(PLANES):
        pack, k = p // 16, p % 16
        to_right = pltpu.roll(rights[pack], 128 - RIM * k, 1) if k else rights[pack]
        turn = (128 - RIM - RIM * k) % 128
        to_left = pltpu.roll(lefts[pack], turn, 1) if turn else lefts[pack]
        out_ref[p, :, COLS:] = jnp.where(on_right, to_right, jnp.where(on_left, to_left, 0.0))

    @pl.when(y == tall - 1)
    def _():
        out_ref[:, ROWS : ROWS + RIM, :COLS] = jnp.zeros((PLANES, RIM, COLS), F32)

    @pl.when(y == 0)
    def _():
        out_ref[:, TALL - RIM :, :COLS] = jnp.zeros((PLANES, RIM, COLS), F32)


def with_halo(velocity, stiffness, mask, thickness, bed, beta):
    return pl.pallas_call(
        halo_kernel,
        name="halo",
        out_shape=jax.ShapeDtypeStruct((PLANES, TALL, LONG), F32),
        in_specs=[VM] * 6,
        out_specs=VM,
        scratch_shapes=[
            pltpu.VMEM((PACKS, ROWS, 128), F32),
            pltpu.VMEM((PACKS, ROWS, 128), F32),
            pltpu.VMEM((PACKS, TALL, 128), F32),
            pltpu.VMEM((PACKS, TALL, 128), F32),
            pltpu.SemaphoreType.DMA((8,)),
            pltpu.SemaphoreType.DMA((8,)),
        ],
        compiler_params=pltpu.CompilerParams(collective_id=5, has_side_effects=True),
    )(velocity.reshape(2 * LEV, ROWS, COLS), stiffness, mask, thickness, bed, beta)


def next_row(a):
    return pltpu.roll(a, a.shape[0] - 1, 0)


def last_row(a):
    return pltpu.roll(a, 1, 0)


def next_col(a):
    return pltpu.roll(a, a.shape[1] - 1, 1)


def last_col(a):
    return pltpu.roll(a, 1, 1)


def folded(a, b):
    inner = a[:ROWS, :COLS] * b[:ROWS, :COLS]
    return inner[0:8] + inner[8:16] + inner[16:24] + inner[24:32]


def apply_level(source, level, gx_ref, gy_ref, gz_ref, mask, friction):
    gx, gy = gx_ref[level], gy_ref[level]
    over, under = gz_ref[level + 1], gz_ref[level]
    upper = jnp.minimum(level + 1, LEV - 1)
    lower = jnp.maximum(level - 1, 0)
    results = []
    for c, (along_x, along_y) in enumerate(((2.0, 0.5), (0.5, 2.0))):
        w = source(c, level)
        held = mask * w
        flow_x = gx * (held - next_row(held))
        flow_y = gy * (held - next_col(held))
        value = along_x * (flow_x - last_row(flow_x)) + along_y * (flow_y - last_col(flow_y))
        value = value + over * (held - mask * source(c, upper)) + under * (held - mask * source(c, lower))
        value = value + friction * held
        results.append(jnp.where(mask > 0.0, value, w))
    return results


def planes_of(ref):
    return lambda c, level: ref[c * LEV + level]


def tile_of(pairs, last=None):
    lane = lax.broadcasted_iota(jnp.int32, (1, 128), 1)
    rows = [jnp.where(lane < 64, a, b) for a, b in pairs]
    rows += [jnp.zeros((1, 128), F32)] * (7 - len(rows))
    rows.append(jnp.zeros((1, 128), F32) if last is None else last)
    return jnp.concatenate(rows, axis=0)


def summed(sums_ref, count):
    return [jnp.sum(sums_ref[i], keepdims=True) for i in range(count)]


def begin_kernel(all_ref, most_ref, r0_ref, v1_ref, v2_ref, gx_ref, gy_ref, gz_ref, part_ref, mu_ref, sums_ref):
    sums_ref[...] = jnp.zeros_like(sums_ref)
    mask = all_ref[MASK]
    beta = all_ref[BETA]

    @pl.loop(0, LEV)
    def _(level):
        upper = jnp.minimum(level + 1, LEV - 1)
        u, v = all_ref[level], all_ref[LEV + level]
        grad_xx = 0.5 * (next_row(u) - last_row(u))
        grad_yy = 0.5 * (next_col(v) - last_col(v))
        cross = 0.5 * (next_col(u) - last_col(u)) + 0.5 * (next_row(v) - last_row(v))
        shear_x = all_ref[upper] - u
        shear_y = all_ref[LEV + upper] - v
        rate = grad_xx * grad_xx + grad_yy * grad_yy + grad_xx * grad_yy
        rate = rate + 0.25 * (cross * cross) + 0.25 * (shear_x * shear_x + shear_y * shear_y)
        base = rate + 0.1
        root = jnp.exp(jnp.log(base) * (-1.0 / 3.0))
        root = root * (4.0 - base * (root * root * root)) * (1.0 / 3.0)
        mu_ref[level] = all_ref[2 * LEV + level] * root

    gz_ref[0] = jnp.zeros((TALL, LONG), F32)
    gz_ref[LEV] = jnp.zeros((TALL, LONG), F32)

    @pl.loop(0, LEV)
    def _(level):
        mu = mu_ref[level]
        gx_ref[level] = mu + next_row(mu)
        gy_ref[level] = mu + next_col(mu)

    @pl.loop(1, LEV)
    def _(level):
        gz_ref[level] = mu_ref[level - 1] + mu_ref[level]

    s0 = all_ref[BED] + all_ref[THICK]
    force = -(mask * all_ref[THICK])
    drive = (force * (0.5 * (next_row(s0) - last_row(s0))), force * (0.5 * (next_col(s0) - last_col(s0))))

    def at_level(level):
        return jnp.where(level == 0, beta, 0.0)

    @pl.loop(0, LEV)
    def _(level):
        for c, value in enumerate(apply_level(planes_of(all_ref), level, gx_ref, gy_ref, gz_ref, mask, at_level(level))):
            r = drive[c] - value
            r0_ref[c * LEV + level] = r
            sums_ref[0] += folded(r, r)

    @pl.loop(0, LEV)
    def _(level):
        for c, value in enumerate(apply_level(planes_of(r0_ref), level, gx_ref, gy_ref, gz_ref, mask, at_level(level))):
            v1_ref[c * LEV + level] = value
            sums_ref[1] += folded(value, r0_ref[c * LEV + level])
            sums_ref[2] += folded(value, value)

    @pl.loop(0, LEV)
    def _(level):
        for c, value in enumerate(apply_level(planes_of(v1_ref), level, gx_ref, gy_ref, gz_ref, mask, at_level(level))):
            v2_ref[c * LEV + level] = value
            sums_ref[3] += folded(value, v1_ref[c * LEV + level])

    part_ref[...] = tile_of([(s, s) for s in summed(sums_ref, 4)], most_ref[:1, :])


def first_scalars(total_ref):
    m0, m1, m2, m3 = (total_ref[i : i + 1, 0:1] for i in range(4))
    a0 = m0 / m1
    rr1 = a0 * a0 * m2 - m0
    b1 = rr1 / m0
    c = 1.0 + b1
    along = c * c * m1 - 2.0 * c * a0 * m2 + a0 * a0 * m3
    a1 = rr1 / along
    return a0, a1, c, rr1, along


def middle_kernel(total_ref, all_ref, r0_ref, v1_ref, v2_ref, gx_ref, gy_ref, gz_ref, s_ref, part_ref, r2_ref, q1_ref, sums_ref):
    a0, a1, c, _, _ = first_scalars(total_ref)
    sums_ref[...] = jnp.zeros_like(sums_ref)
    mask = all_ref[MASK]
    beta = all_ref[BETA]

    @pl.loop(0, 2 * LEV)
    def _(p):
        v1 = v1_ref[p]
        q1 = c * v1 - a0 * v2_ref[p]
        r2 = r0_ref[p] - a0 * v1 - a1 * q1
        q1_ref[p] = q1
        r2_ref[p] = r2
        sums_ref[0] += folded(r2, r2)
        sums_ref[1] += folded(r2, q1)
        sums_ref[2] += folded(q1, q1)

    def at_level(level):
        return jnp.where(level == 0, beta, 0.0)

    @pl.loop(0, LEV)
    def _(level):
        for c, value in enumerate(apply_level(planes_of(r2_ref), level, gx_ref, gy_ref, gz_ref, mask, at_level(level))):
            p = c * LEV + level
            s_ref[p] = value
            sums_ref[3] += folded(value, r2_ref[p])
            sums_ref[4] += folded(value, value)
            sums_ref[5] += folded(value, q1_ref[p])

    @pl.loop(0, LEV)
    def _(level):
        for c, value in enumerate(apply_level(planes_of(q1_ref), level, gx_ref, gy_ref, gz_ref, mask, at_level(level))):
            sums_ref[6] += folded(value, q1_ref[c * LEV + level])

    @pl.loop(0, LEV)
    def _(level):
        for c, value in enumerate(apply_level(planes_of(s_ref), level, gx_ref, gy_ref, gz_ref, mask, at_level(level))):
            p = c * LEV + level
            sums_ref[7] += folded(value, s_ref[p])
            sums_ref[8] += folded(value, q1_ref[p])

    d = summed(sums_ref, 9)
    part_ref[...] = tile_of([(d[0], d[1]), (d[2], d[3]), (d[4], d[5]), (d[6], d[7]), (d[8], d[8])])


def end_kernel(first_ref, second_ref, all_ref, r0_ref, v1_ref, v2_ref, s_ref, velocity_ref, spread_ref):
    a0, a1, c, rr1, pq = first_scalars(first_ref)
    pair = lambda i: (second_ref[i : i + 1, 0:1], second_ref[i : i + 1, 64:65])
    (rr2, rq), (qq, rs), (ss, sq), (tq, su), (uq, _) = (pair(i) for i in range(5))
    b = rr2 / rr1
    p2q2 = rs + 2.0 * b * rq + b * b * pq
    a2 = rr2 / p2q2
    r2q2 = rs + b * rq
    q2q2 = ss + 2.0 * b * sq + b * b * qq
    rr3 = rr2 - 2.0 * a2 * r2q2 + a2 * a2 * q2q2
    b3 = rr3 / rr2
    q2t2 = su + 2.0 * b * uq + b * b * tq
    p3q3 = (
        rs
        - 2.0 * a2 * (ss + b * sq)
        + a2 * a2 * q2t2
        + 2.0 * b3 * (r2q2 - a2 * q2q2)
        + b3 * b3 * p2q2
    )
    a3 = rr3 / p3q3
    of_p2 = a2 + a3 * b3
    of_r2 = of_p2 + a3
    of_p1 = of_p2 * b + a1
    of_s = -(a3 * a2)
    of_q1 = of_s * b - of_r2 * a1
    of_r0 = a0 + of_p1 * c + of_r2
    of_v1 = of_q1 * c - of_p1 * a0 - of_r2 * a0
    of_v2 = -(of_q1 * a0)

    means = []
    for k in range(2):
        mean = jnp.zeros((TALL, LONG), F32)
        for level in range(LEV):
            p = k * LEV + level
            value = all_ref[p] + of_r0 * r0_ref[p] + of_v1 * v1_ref[p] + of_v2 * v2_ref[p] + of_s * s_ref[p]
            velocity_ref[p] = value[:ROWS, :COLS]
            mean = mean + value
        means.append(all_ref[THICK] * (mean * (1.0 / LEV)))
    spread = 0.5 * (next_row(means[0]) - last_row(means[0])) + 0.5 * (next_col(means[1]) - last_col(means[1]))
    spread_ref[...] = spread[:ROWS, :COLS]


def solve(padded, most):
    block = jax.ShapeDtypeStruct((2 * LEV, TALL, LONG), F32)
    tile = jax.ShapeDtypeStruct((8, 128), F32)
    level = jax.ShapeDtypeStruct((LEV, TALL, LONG), F32)
    room = pltpu.CompilerParams(vmem_limit_bytes=56 << 20)
    r0, v1, v2, gx, gy, gz, part = pl.pallas_call(
        begin_kernel,
        name="begin",
        out_shape=(block, block, block, level, level, jax.ShapeDtypeStruct((LEV + 1, TALL, LONG), F32), tile),
        in_specs=[VM] * 2,
        out_specs=(VM,) * 7,
        scratch_shapes=[pltpu.VMEM((LEV, TALL, LONG), F32), pltpu.VMEM((4, 8, COLS), F32)],
        compiler_params=room,
    )(padded, most)
    first = total(part, "total_first", 1)
    s, part = pl.pallas_call(
        middle_kernel,
        name="middle",
        out_shape=(block, tile),
        in_specs=[VM] * 8,
        out_specs=(VM,) * 2,
        scratch_shapes=[pltpu.VMEM((2 * LEV, TALL, LONG), F32)] * 2 + [pltpu.VMEM((9, 8, COLS), F32)],
        compiler_params=room,
    )(first, padded, r0, v1, v2, gx, gy, gz)
    second = total(part, "total_second", 6)
    velocity, spread = pl.pallas_call(
        end_kernel,
        name="end",
        out_shape=(
            jax.ShapeDtypeStruct((2 * LEV, ROWS, COLS), F32),
            jax.ShapeDtypeStruct((ROWS, COLS), F32),
        ),
        in_specs=[VM] * 7,
        out_specs=(VM,) * 2,
        compiler_params=room,
    )(first, second, padded, r0, v1, v2, s)
    return velocity.reshape(2, LEV, ROWS, COLS), spread, first[7, 0]


def on_device(
    velocity_start,
    stiffness,
    beta,
    ice_mask,
    thickness,
    bed,
    land_smb,
    elev_class,
    correlation_cols,
    correlation_weights,
):
    rows, cols = bed.shape
    own_table = land_smb.reshape(-1, 128)

    def turn(number):
        return route(
            jnp.full((1,), number, jnp.int32), correlation_cols, elev_class, correlation_weights
        )

    def balance_and_weights(send, cell, got, swap):
        denom, found = owner(own_table, got)
        return scatter(cell, send, swap(found)), denom

    def plain_swap(array):
        return lax.all_to_all(array, ("ty", "tx"), 0, 0, tiled=True)

    send, cell, most = turn(0)
    got = exchange(send, "to_owner", 2)
    smb_ice, denom = balance_and_weights(send, cell, got, lambda a: exchange(a, "from_owner", 3))

    padded = with_halo(velocity_start, stiffness, ice_mask, thickness, bed, beta)
    velocity, spread, most = solve(padded, most)
    turns = ((most.astype(jnp.int32) + SLOTS - 1) // SLOTS).astype(jnp.int32)

    def more_balance(carry):
        number, smb, weights = carry
        send, cell, _ = turn(number)
        add_smb, add_weights = balance_and_weights(send, cell, plain_swap(send), plain_swap)
        return number + 1, smb + add_smb, weights + add_weights

    def unfinished(carry):
        return carry[0] < turns

    _, smb_ice, denom = lax.while_loop(unfinished, more_balance, (jnp.int32(1), smb_ice, denom))
    surface = bed + thickness + 0.5 * (smb_ice.reshape(rows, cols) - spread)
    surface_rows = surface.reshape(-1, 128)
    numer = scatter(got, got, exchange(gather(surface_rows, cell), "to_land", 4))

    def more_numer(carry):
        number, numer = carry
        send, cell, _ = turn(number)
        got = plain_swap(send)
        return number + 1, numer + scatter(got, got, plain_swap(gather(surface_rows, cell)))

    _, numer = lax.while_loop(unfinished, more_numer, (jnp.int32(1), numer))
    used = own_table.shape[0]
    land_surface = (numer[:used] / (denom[:used] + 1.0)).reshape(land_smb.shape)
    return (velocity, surface, land_surface)


def solution(mesh):
    every = ("ty", "tx")
    return jax.shard_map(
        on_device,
        mesh=mesh,
        in_specs=(
            P(None, None, "ty", "tx"),
            P(None, "ty", "tx"),
            P("ty", "tx"),
            P("ty", "tx"),
            P("ty", "tx"),
            P("ty", "tx"),
            P(None, every),
            P("ty", "tx"),
            P(None, "ty", "tx"),
            P(None, "ty", "tx"),
        ),
        out_specs=(P(None, None, "ty", "tx"), P("ty", "tx"), P(None, every)),
        check_vma=False,
    )
```

profile of v0, /device:TPU:25, one launch (start us, length us, event | category | flops | bytes accessed | tf_op | source)
XLA Modules:
  0.0 210.5 jit_solution(17917338895180671859)
XLA Ops:
  0.7 16.9 %halo.1.all_ref = f32[34,48,384]{2,1,0:T(8,128)} custom-call(f32[20,32,256]{2,1,0:T(8,128)} %bitcast.29, f32[10,32,256]{2,1,0:T(8,128)} %stiff_ref.1, s32[32,256]{1,0:T(8,128)} %mask_ref.1, f32[32,256]{1,0:T(8,128)} %thick_ref.1, f32[32,256]{1,0:T(8,128)} %bed_ref.1, f32[32,256]{1,0:T(8,128)} %beta_ref.1), custom_call_target="tpu_custom_call" | custom-call | tf_op jit(solution)/shard_map/halo/pallas_call | solution.py:426
  17.6 27.3 %route.3 = (f32[128,8,128]{2,1,0:T(8,128)S(1)}, f32[128,4,128]{2,1,0:T(4,128)S(1)}, f32[8,128]{1,0:T(8,128)S(1)}) custom-call(s32[1]{0:T(128)} %constant.22.clone.1.turn_ref, s32[128,256]{1,0:T(8,128)S(1)} %bitcast.23, s32[32,256]{1,0:T(8,128)S(1)} %copy-done.11, f32[128,256]{1,0:T(8,128)S(1)} %bitcast.26), custom_call_target="tpu_custom_call" | custom-call | tf_op jit(solution)/shard_map/route/pallas_call | solution.py:85
  45.0 0.8 copy-done.2
  45.8 0.6 copy-done.8
  46.4 15.0 %begin.1 = (f32[20,48,384]{2,1,0:T(8,128)}, f32[20,48,384]{2,1,0:T(8,128)}, f32[20,48,384]{2,1,0:T(8,128)}, f32[10,48,384]{2,1,0:T(8,128)}, f32[10,48,384]{2,1,0...) custom-call(f32[34,48,384]{2,1,0:T(8,128)} %halo.1.all_ref, f32[8,128]{1,0:T(8,128)} %copy-done.8), custom_call_target="tpu_custom_call" | custom-call | tf_op jit(solution)/shard_map/begin/pallas_call | solution.py:666
  61.4 12.2 %total_first.1.total_ref.first_ref = f32[8,128]{1,0:T(8,128)} custom-call(f32[8,128]{1,0:T(8,128)} %get-tuple-element.108.part_ref), custom_call_target="tpu_custom_call" | custom-call | tf_op jit(solution)/shard_map/total_first/pallas_call | solution.py:327
  73.5 12.1 %middle.1 = (f32[20,48,384]{2,1,0:T(8,128)}, f32[8,128]{1,0:T(8,128)}) custom-call(f32[8,128]{1,0:T(8,128)} %total_first.1.total_ref.first_ref, f32[34,48,384]{2,1,0:T(8,128)} %halo.1.all_ref, f32[20,48,384]{2,1,0:T(8,128)} %get-tuple-element.109.r0_ref, f32[20,48,384]{2,1,0:T(8,128)} %get-tuple-element.110.v1_ref, ...), custom_call_target="tpu_custom_call" | custom-call | tf_op jit(solution)/shard_map/middle/pallas_call | solution.py:676
  85.6 12.8 %total_second.1.second_ref = f32[8,128]{1,0:T(8,128)} custom-call(f32[8,128]{1,0:T(8,128)} %get-tuple-element.115.part_ref), custom_call_target="tpu_custom_call" | custom-call | tf_op jit(solution)/shard_map/total_second/pallas_call | solution.py:327
  98.4 0.0 copy-start.16
  98.5 5.1 %end.1 = (f32[20,32,256]{2,1,0:T(8,128)}, f32[32,256]{1,0:T(8,128)}) custom-call(f32[8,128]{1,0:T(8,128)} %total_first.1.total_ref.first_ref, f32[8,128]{1,0:T(8,128)} %total_second.1.second_ref, f32[34,48,384]{2,1,0:T(8,128)} %halo.1.all_ref, f32[20,48,384]{2,1,0:T(8,128)} %get-tuple-element.109.r0_ref, f32[20,48,384]{2,1,0:T(8,128)} %get-tuple-element.110.v1_ref, ...), custom_call_target="tpu_custom_call" | custom-call | tf_op jit(solution)/shard_map/end/pallas_call | solution.py:686
  103.6 18.4 %to_owner.1.got_ref.where_ref.weights_ref = f32[128,8,128]{2,1,0:T(8,128)} custom-call(f32[128,8,128]{2,1,0:T(8,128)} %copy-done.2), custom_call_target="tpu_custom_call" | custom-call | tf_op jit(solution)/shard_map/to_owner/pallas_call | solution.py:272
  122.1 1.0 copy-done
  123.1 18.7 %owner.2 = (f32[64,128]{1,0:T(8,128)S(1)}, f32[128,4,128]{2,1,0:T(4,128)S(1)}) custom-call(f32[40,128]{1,0:T(8,128)S(1)} %reshape.49.table_ref, f32[128,8,128]{2,1,0:T(8,128)S(1)} %copy-done), custom_call_target="tpu_custom_call" | custom-call | tf_op jit(solution)/shard_map/owner/pallas_call | solution.py:161
  141.8 0.7 copy-done.7
  142.5 15.7 %from_owner.1.values_ref = f32[128,4,128]{2,1,0:T(4,128)} custom-call(f32[128,4,128]{2,1,0:T(4,128)} %copy-done.7), custom_call_target="tpu_custom_call" | custom-call | tf_op jit(solution)/shard_map/from_owner/pallas_call | solution.py:272
  158.2 0.9 copy-done.5
  159.2 10.5 %put.4 = f32[64,128]{1,0:T(8,128)S(1)} custom-call(f32[128,4,128]{2,1,0:T(4,128)S(1)} %get-tuple-element.118.where_ref, f32[128,8,128]{2,1,0:T(8,128)S(1)} %copy-done.3, f32[128,4,128]{2,1,0:T(4,128)S(1)} %copy-done.5), custom_call_target="tpu_custom_call" | custom-call | tf_op jit(solution)/shard_map/put/pallas_call | solution.py:219
  169.6 1.2 slice.9
  171.5 0.0 copy-start.12
  171.5 0.0 copy-start.15
  171.5 0.2 while.22
  171.7 0.5 copy-done.12
  172.2 0.0 copy-done.13
  172.3 0.0 copy-done.15
  172.3 0.0 copy-start.14
  172.3 10.0 %pick.2.send_ref = f32[128,4,128]{2,1,0:T(4,128)S(1)} custom-call(f32[64,128]{1,0:T(8,128)S(1)} %reshape.51.table_ref, f32[128,4,128]{2,1,0:T(4,128)S(1)} %get-tuple-element.118.where_ref), custom_call_target="tpu_custom_call" | custom-call | tf_op jit(solution)/shard_map/pick/pallas_call | solution.py:188
  182.3 0.7 copy-done.4
  183.0 15.2 %to_land.1.values_ref = f32[128,4,128]{2,1,0:T(4,128)} custom-call(f32[128,4,128]{2,1,0:T(4,128)} %copy-done.4), custom_call_target="tpu_custom_call" | custom-call | tf_op jit(solution)/shard_map/to_land/pallas_call | solution.py:272
  198.2 0.9 copy-done.6
  199.2 10.5 %put.5 = f32[64,128]{1,0:T(8,128)S(1)} custom-call(f32[128,8,128]{2,1,0:T(8,128)S(1)} %copy-done.1, f32[128,8,128]{2,1,0:T(8,128)S(1)} %copy-done.1, f32[128,4,128]{2,1,0:T(4,128)S(1)} %copy-done.6), custom_call_target="tpu_custom_call" | custom-call | tf_op jit(solution)/shard_map/put/pallas_call | solution.py:219
  209.7 0.2 while.23
  209.9 0.6 reshape.52
  (25 shorter events, 0.1 us)
Async XLA Ops:
  0.6 17.0 %copy-start.9 = (s32[4,32,256]{2,1,0:T(8,128)S(1)}, s32[4,32,256]{2,1,0:T(8,128)}, u32[]{:S(2)}) copy-start(s32[4,32,256]{2,1,0:T(8,128)} %param.22) | copy-start | bytes 393220
  0.6 17.0 %copy-start.10 = (f32[4,32,256]{2,1,0:T(8,128)S(1)}, f32[4,32,256]{2,1,0:T(8,128)}, u32[]{:S(2)}) copy-start(f32[4,32,256]{2,1,0:T(8,128)} %param.23) | copy-start | bytes 393220
  0.7 17.0 %copy-start.11 = (s32[32,256]{1,0:T(8,128)S(1)}, s32[32,256]{1,0:T(8,128)}, u32[]{:S(2)}) copy-start(s32[32,256]{1,0:T(8,128)} %class_ref.1) | copy-start | bytes 98308
  45.0 0.8 copy-start.2
  45.8 0.6 copy-start.8
  98.4 5.1 %copy-start.16 = (f32[10,512]{1,0:T(8,128)S(1)}, f32[10,512]{1,0:T(8,128)}, u32[]{:S(2)}) copy-start(f32[10,512]{1,0:T(8,128)} %param.20) | copy-start | bytes 61444
  103.6 54.6 %copy-start.3 = (f32[128,8,128]{2,1,0:T(8,128)S(1)}, f32[128,8,128]{2,1,0:T(8,128)}, u32[]{:S(2)}) copy-start(f32[128,8,128]{2,1,0:T(8,128)} %copy-done.2) | copy-start | bytes 1572868
  122.1 1.0 copy-start
  141.8 0.7 copy-start.7
  158.2 1.0 copy-start.5
  171.5 0.8 copy-start.12
  171.5 0.8 copy-start.13
  171.5 0.8 copy-start.15
  171.7 26.5 %copy-start.1 = (f32[128,8,128]{2,1,0:T(8,128)S(1)}, f32[128,8,128]{2,1,0:T(8,128)}, u32[]{:S(2)}) copy-start(f32[128,8,128]{2,1,0:T(8,128)} %to_owner.1.got_ref.where_ref.weights_ref) | copy-start | bytes 1572868
  172.3 37.3 %copy-start.14 = (f32[32,256]{1,0:T(8,128)}, f32[32,256]{1,0:T(8,128)S(1)}, u32[]{:S(2)}) copy-start(f32[32,256]{1,0:T(8,128)S(1)} %multiply_add_fusion) | copy-start | bytes 98308
  182.3 0.7 copy-start.4
  198.2 1.0 copy-start.6
where the time goes:
time: 213 us; the launch traced here: 211 us
  Pallas kernels  200 us (94%)
  local copies, waits for them, and re-layouts  8.13 us (4%)
    pallas_call x3, Pallas kernels, exchange(): pl.pallas_call(exchange_kernel, name=name, out_shape=jax.ShapeDtypeStruct...  49.3 us
    pallas_call x1, Pallas kernels, route(): pl.pallas_call(functools.partial(route_kernel, peers), name='route', out_...  27.3 us
    pallas_call x2, Pallas kernels, total(): pl.pallas_call(total_kernel, name=name, out_shape=jax.ShapeDtypeStruct(sh...  24.9 us
    pallas_call x2, Pallas kernels, scatter(): pl.pallas_call(functools.partial(scatter_kernel, 0), name='put', out_shap...  20.9 us
    pallas_call x1, Pallas kernels, owner(): pl.pallas_call(owner_kernel, name='owner', out_shape=(jax.ShapeDtypeStruc...  18.7 us
    pallas_call x1, Pallas kernels, with_halo(): pl.pallas_call(halo_kernel, name='halo', out_shape=jax.ShapeDtypeStruct((...  16.9 us
    pallas_call x1, Pallas kernels, solve(): pl.pallas_call(begin_kernel, name='begin', out_shape=(block, block, block...  15 us
    pallas_call x1, Pallas kernels, solve(): pl.pallas_call(middle_kernel, name='middle', out_shape=(block, tile), in_...  12.1 us

commit v1 on v0

--- a/solution.py
+++ b/solution.py
@@ -40,7 +40,7 @@
         jnp.int32, (width, 2 * width), 1
     )
     ahead = jnp.where(before, 1.0, 0.0).astype(BF)
-    first = turn_ref[0] * SLOTS
+    first = 0 if turn_ref is None else turn_ref[0] * SLOTS
     most = jnp.zeros((peers, width), F32)
     for k in range(4):
         total_ref[...] = jnp.zeros_like(total_ref)
@@ -52,7 +52,7 @@
             dest = cols >> 9
             lane = lax.broadcasted_iota(jnp.int32, cols.shape, 1)
             row = lax.broadcasted_iota(jnp.int32, cols.shape, 0) + g * step
-            whole = (kind * 4 + ((cols >> 7) & 3), cols & 127, row * 2 + (lane >> 7), lane & 127)
+            whole = (kind * 4 + ((cols >> 7) & 3), cols & 127, (lane >> 7) * 32 + row, lane & 127)
             fields = [v.astype(F32) for v in whole]
             w = weights_ref[pl.ds(at, step), :]
             w_top = w.astype(BF).astype(F32)
@@ -133,25 +133,54 @@
     return [tiles[s, k : k + 1, :] for s in range(tiles.shape[0]) for k in range(4)]
 
 
+def owner_group(g, got_ref, terms_ref, total_ref, back_ref):
+    tile = got_ref[pl.ds(g * GROUP, GROUP), :, :]
+    high, low = spots(tile[:, :4, :])
+    w = across(flat_rows(tile[:, 4:, :]))
+    high_hot = hot(HIGH, across(flat_rows(high)))
+    low_mask = is_row(128, across(flat_rows(low)))
+    low_hot = jnp.where(low_mask, 1.0, 0.0).astype(BF)
+    w_top = w.astype(BF).astype(F32)
+    add_in(total_ref, (w_top, w - w_top), high_hot, low_hot)
+    found = look_up(terms_ref[...], high_hot, low_mask)
+    put_rows(back_ref, g, found)
+
+
+def put_rows(out_ref, g, found):
+    for s in range(GROUP):
+        for k in range(4):
+            i = s * 4 + k
+            out_ref[g * GROUP + s, k : k + 1, :] = found[:, i * 128 : (i + 1) * 128]
+
+
+def gather_group(g, terms_ref, where_ref, out_ref):
+    high, low = spots(where_ref[pl.ds(g * GROUP, GROUP), :, :])
+    found = look_up(
+        terms_ref[...], hot(HIGH, across(flat_rows(high))), is_row(128, across(flat_rows(low)))
+    )
+    put_rows(out_ref, g, found)
+
+
+def scatter_group(g, where_ref, weights_ref, values_ref, total_ref):
+    span = pl.ds(g * GROUP, GROUP)
+    high, low = spots(where_ref[span, :4, :])
+    v = across(flat_rows(weights_ref[span, 4:, :] * values_ref[span, :, :]))
+    v_top = v.astype(BF).astype(F32)
+    add_in(
+        total_ref,
+        (v_top, v - v_top),
+        hot(HIGH, across(flat_rows(high))),
+        hot(128, across(flat_rows(low))),
+    )
+
+
 def owner_kernel(table_ref, got_ref, denom_ref, back_ref, terms_ref, total_ref):
     terms_ref[...] = table_terms(table_ref[...])
     total_ref[...] = jnp.zeros_like(total_ref)
 
     @pl.loop(0, got_ref.shape[0] // GROUP)
     def _(g):
-        tile = got_ref[pl.ds(g * GROUP, GROUP), :, :]
-        high, low = spots(tile[:, :4, :])
-        w = across(flat_rows(tile[:, 4:, :]))
-        high_hot = hot(HIGH, across(flat_rows(high)))
-        low_mask = is_row(128, across(flat_rows(low)))
-        low_hot = jnp.where(low_mask, 1.0, 0.0).astype(BF)
-        w_top = w.astype(BF).astype(F32)
-        add_in(total_ref, (w_top, w - w_top), high_hot, low_hot)
-        found = look_up(terms_ref[...], high_hot, low_mask)
-        for s in range(GROUP):
-            for k in range(4):
-                i = s * 4 + k
-                back_ref[g * GROUP + s, k : k + 1, :] = found[:, i * 128 : (i + 1) * 128]
+        owner_group(g, got_ref, terms_ref, total_ref, back_ref)
 
     denom_ref[...] = total_ref[:HIGH, :] + total_ref[HIGH:, :]
 
@@ -174,14 +203,7 @@
 
     @pl.loop(0, where_ref.shape[0] // GROUP)
     def _(g):
-        high, low = spots(where_ref[pl.ds(g * GROUP, GROUP), :, :])
-        found = look_up(
-            terms_ref[...], hot(HIGH, across(flat_rows(high))), is_row(128, across(flat_rows(low)))
-        )
-        for s in range(GROUP):
-            for k in range(4):
-                i = s * 4 + k
-                out_ref[g * GROUP + s, k : k + 1, :] = found[:, i * 128 : (i + 1) * 128]
+        gather_group(g, terms_ref, where_ref, out_ref)
 
 
 def gather(table, where):
@@ -196,28 +218,19 @@
     )(table, where)
 
 
-def scatter_kernel(first, where_ref, weights_ref, values_ref, out_ref, total_ref):
+def scatter_kernel(where_ref, weights_ref, values_ref, out_ref, total_ref):
     total_ref[...] = jnp.zeros_like(total_ref)
 
     @pl.loop(0, where_ref.shape[0] // GROUP)
     def _(g):
-        span = pl.ds(g * GROUP, GROUP)
-        high, low = spots(where_ref[span, :4, :])
-        v = across(flat_rows(weights_ref[span, 4:, :] * values_ref[span, :, :]))
-        v_top = v.astype(BF).astype(F32)
-        add_in(
-            total_ref,
-            (v_top, v - v_top),
-            hot(HIGH, across(flat_rows(high))),
-            hot(128, across(flat_rows(low))),
-        )
+        scatter_group(g, where_ref, weights_ref, values_ref, total_ref)
 
     out_ref[...] = total_ref[:HIGH, :] + total_ref[HIGH:, :]
 
 
 def scatter(where, weights, values):
     return pl.pallas_call(
-        functools.partial(scatter_kernel, 0),
+        scatter_kernel,
         name="put",
         out_shape=jax.ShapeDtypeStruct((HIGH, 128), F32),
         in_specs=[VM, VM, VM],
@@ -235,109 +248,6 @@
 def at(peer):
     wide = lax.axis_size("tx")
     return (peer // wide, peer % wide)
-
-
-def meet(me, peers):
-    barrier = pltpu.get_barrier_semaphore()
-
-    @pl.loop(1, peers)
-    def _(step):
-        pl.semaphore_signal(barrier, inc=1, device_id=at((me + step) % peers), device_id_type=MESH)
-
-    pl.semaphore_wait(barrier, peers - 1)
-
-
-def exchange_kernel(send_ref, got_ref, out_sem, in_sem, own_sem):
-    me, peers = place()
-    own = pltpu.make_async_copy(send_ref.at[me], got_ref.at[me], own_sem)
-    own.start()
-    meet(me, peers)
-
-    @pl.loop(1, peers)
-    def _(step):
-        peer = (me + step) % peers
-        pltpu.make_async_remote_copy(
-            send_ref.at[peer], got_ref.at[me], out_sem, in_sem, device_id=at(peer), device_id_type=MESH
-        ).start()
-
-    own.wait()
-    others = pl.ds(0, peers - 1)
-    whole = pltpu.make_async_remote_copy(
-        send_ref.at[others], got_ref.at[others], out_sem, in_sem, device_id=at((me + 1) % peers), device_id_type=MESH
-    )
-    whole.wait()
-
-
-def exchange(send, name, number):
-    return pl.pallas_call(
-        exchange_kernel,
-        name=name,
-        out_shape=jax.ShapeDtypeStruct(send.shape, send.dtype),
-        in_specs=[VM],
-        out_specs=VM,
-        scratch_shapes=[pltpu.SemaphoreType.DMA] * 3,
-        compiler_params=pltpu.CompilerParams(collective_id=number, has_side_effects=True),
-    )(send)
-
-
-def joined(tiles):
-    row = lax.broadcasted_iota(jnp.int32, tiles.shape[1:], 0)
-    return jnp.where(row < 7, jnp.sum(tiles, axis=0), jnp.max(tiles, axis=0))
-
-
-def total_kernel(part_ref, sum_ref, near_ref, half_ref, far_ref, near_out, near_in, far_out, far_in):
-    y, x = lax.axis_index("ty"), lax.axis_index("tx")
-    tall, wide = lax.axis_size("ty"), lax.axis_size("tx")
-    core, chip = x % 2, x // 2
-    near, far = tall * 2, wide // 2
-    me = y * 2 + core
-    near_ids = [(me + i) % near for i in range(1, near)]
-    near_devices = [(i // 2, chip * 2 + i % 2) for i in near_ids]
-    far_devices = [(y, ((chip + i) % far) * 2 + core) for i in range(1, far)]
-    barrier = pltpu.get_barrier_semaphore()
-    for device in near_devices + far_devices:
-        pl.semaphore_signal(barrier, inc=1, device_id=device, device_id_type=MESH)
-    pl.semaphore_wait(barrier, near + far - 2)
-    for device in near_devices:
-        pltpu.make_async_remote_copy(
-            part_ref, near_ref.at[me], near_out, near_in, device_id=device, device_id_type=MESH
-        ).start()
-    near_ref[pl.ds(me, 1)] = part_ref[...][None]
-    whole = pl.ds(0, near - 1)
-    pltpu.make_async_remote_copy(
-        near_ref.at[whole], near_ref.at[whole], near_out, near_in, device_id=near_devices[0], device_id_type=MESH
-    ).wait()
-    half = joined(near_ref[...])
-    half_ref[...] = half
-    for device in far_devices:
-        pltpu.make_async_remote_copy(
-            half_ref, far_ref.at[chip], far_out, far_in, device_id=device, device_id_type=MESH
-        ).start()
-    far_ref[pl.ds(chip, 1)] = half[None]
-    whole = pl.ds(0, far - 1)
-    pltpu.make_async_remote_copy(
-        far_ref.at[whole], far_ref.at[whole], far_out, far_in, device_id=far_devices[0], device_id_type=MESH
-    ).wait()
-    sum_ref[...] = joined(far_ref[...])
-
-
-def total(part, name, number):
-    tall, wide = lax.axis_size("ty"), lax.axis_size("tx")
-    shape = part.shape
-    return pl.pallas_call(
-        total_kernel,
-        name=name,
-        out_shape=jax.ShapeDtypeStruct(shape, part.dtype),
-        in_specs=[VM],
-        out_specs=VM,
-        scratch_shapes=[
-            pltpu.VMEM((tall * 2, *shape), part.dtype),
-            pltpu.VMEM(shape, part.dtype),
-            pltpu.VMEM((wide // 2, *shape), part.dtype),
-        ]
-        + [pltpu.SemaphoreType.DMA] * 4,
-        compiler_params=pltpu.CompilerParams(collective_id=number, has_side_effects=True),
-    )(part)
 
 
 LEV = 10
@@ -350,9 +260,8 @@
 ALL_ROWS = pl.ds(0, ROWS)
 
 
-def halo_kernel(vel_ref, stiff_ref, mask_ref, thick_ref, bed_ref, beta_ref, out_ref, left_ref, right_ref, from_right, from_left, out_sem, in_sem):
-    y, x = lax.axis_index("ty"), lax.axis_index("tx")
-    tall, wide = lax.axis_size("ty"), lax.axis_size("tx")
+def pack_halo(fields, all_ref, left_ref, right_ref, each):
+    vel_ref, stiff_ref, mask_ref, thick_ref, bed_ref, beta_ref = fields
     lane = lax.broadcasted_iota(jnp.int32, (ROWS, 128), 1)
     left = [jnp.zeros((ROWS, 128), F32)] * PACKS
     right = [jnp.zeros((ROWS, 128), F32)] * PACKS
@@ -365,40 +274,45 @@
             plane = mask_ref[...].astype(F32)
         else:
             plane = {THICK: thick_ref, BED: bed_ref, BETA: beta_ref}[p][...]
-        out_ref[p, :ROWS, :COLS] = plane
+        all_ref[p, :ROWS, :COLS] = plane
         pack, k = p // 16, p % 16
         here = (lane >= RIM * k) & (lane < RIM * (k + 1))
         first, last = plane[:, :128], plane[:, COLS - 128 :]
         left[pack] = jnp.where(here, pltpu.roll(first, RIM * k, 1) if k else first, left[pack])
         turn = (RIM * k + RIM) % 128
         right[pack] = jnp.where(here, pltpu.roll(last, turn, 1) if turn else last, right[pack])
+        each(p)
     for i in range(PACKS):
         left_ref[i] = left[i]
         right_ref[i] = right[i]
+
+
+def halo_copies(all_ref, left_ref, right_ref, from_right, from_left, out_sem, in_sem):
+    y, x = lax.axis_index("ty"), lax.axis_index("tx")
+    tall, wide = lax.axis_size("ty"), lax.axis_size("tx")
     around = [(a, b) for a in (-1, 0, 1) for b in (-1, 0, 1) if (a, b) != (0, 0)]
-    where = [((y + a + tall) % tall, (x + b + wide) % wide) for a, b in around]
-    barrier = pltpu.get_barrier_semaphore()
-    for device in where:
-        pl.semaphore_signal(barrier, inc=1, device_id=device, device_id_type=MESH)
-    pl.semaphore_wait(barrier, len(where))
     copies = []
-    for i, ((a, b), device) in enumerate(zip(around, where)):
+    for i, (a, b) in enumerate(around):
         rows = {-1: pl.ds(0, RIM), 0: ALL_ROWS, 1: pl.ds(ROWS - RIM, RIM)}[a]
         there = {-1: pl.ds(ROWS, RIM), 0: ALL_ROWS, 1: pl.ds(TALL - RIM, RIM)}[a]
         if b == 0:
-            ends = out_ref.at[:, rows, pl.ds(0, COLS)], out_ref.at[:, there, pl.ds(0, COLS)]
+            ends = all_ref.at[:, rows, pl.ds(0, COLS)], all_ref.at[:, there, pl.ds(0, COLS)]
         elif b < 0:
             ends = left_ref.at[:, rows, :], from_right.at[:, there, :]
         else:
             ends = right_ref.at[:, rows, :], from_left.at[:, there, :]
+        device = ((y + a + tall) % tall, (x + b + wide) % wide)
         copies.append(
             pltpu.make_async_remote_copy(
                 *ends, out_sem.at[i], in_sem.at[i], device_id=device, device_id_type=MESH
             )
         )
-        copies[-1].start()
-    for copy in copies:
-        copy.wait()
+    return copies
+
+
+def unpack_halo(all_ref, from_right, from_left):
+    y, x = lax.axis_index("ty"), lax.axis_index("tx")
+    tall, wide = lax.axis_size("ty"), lax.axis_size("tx")
     row = lax.broadcasted_iota(jnp.int32, (TALL, 128), 0)
     lane = lax.broadcasted_iota(jnp.int32, (TALL, 128), 1)
     inside = (row < ROWS) | ((row < ROWS + RIM) & (y < tall - 1)) | ((row >= TALL - RIM) & (y > 0))
@@ -411,34 +325,15 @@
         to_right = pltpu.roll(rights[pack], 128 - RIM * k, 1) if k else rights[pack]
         turn = (128 - RIM - RIM * k) % 128
         to_left = pltpu.roll(lefts[pack], turn, 1) if turn else lefts[pack]
-        out_ref[p, :, COLS:] = jnp.where(on_right, to_right, jnp.where(on_left, to_left, 0.0))
+        all_ref[p, :, COLS:] = jnp.where(on_right, to_right, jnp.where(on_left, to_left, 0.0))
 
     @pl.when(y == tall - 1)
     def _():
-        out_ref[:, ROWS : ROWS + RIM, :COLS] = jnp.zeros((PLANES, RIM, COLS), F32)
+        all_ref[:, ROWS : ROWS + RIM, :COLS] = jnp.zeros((PLANES, RIM, COLS), F32)
 
     @pl.when(y == 0)
     def _():
-        out_ref[:, TALL - RIM :, :COLS] = jnp.zeros((PLANES, RIM, COLS), F32)
-
-
-def with_halo(velocity, stiffness, mask, thickness, bed, beta):
-    return pl.pallas_call(
-        halo_kernel,
-        name="halo",
-        out_shape=jax.ShapeDtypeStruct((PLANES, TALL, LONG), F32),
-        in_specs=[VM] * 6,
-        out_specs=VM,
-        scratch_shapes=[
-            pltpu.VMEM((PACKS, ROWS, 128), F32),
-            pltpu.VMEM((PACKS, ROWS, 128), F32),
-            pltpu.VMEM((PACKS, TALL, 128), F32),
-            pltpu.VMEM((PACKS, TALL, 128), F32),
-            pltpu.SemaphoreType.DMA((8,)),
-            pltpu.SemaphoreType.DMA((8,)),
-        ],
-        compiler_params=pltpu.CompilerParams(collective_id=5, has_side_effects=True),
-    )(velocity.reshape(2 * LEV, ROWS, COLS), stiffness, mask, thickness, bed, beta)
+        all_ref[:, TALL - RIM :, :COLS] = jnp.zeros((PLANES, RIM, COLS), F32)
 
 
 def next_row(a):
@@ -496,13 +391,14 @@
     return [jnp.sum(sums_ref[i], keepdims=True) for i in range(count)]
 
 
-def begin_kernel(all_ref, most_ref, r0_ref, v1_ref, v2_ref, gx_ref, gy_ref, gz_ref, part_ref, mu_ref, sums_ref):
+def begin(each, all_ref, most_ref, r0_ref, v1_ref, v2_ref, gx_ref, gy_ref, gz_ref, part_ref, mu_ref, sums_ref):
     sums_ref[...] = jnp.zeros_like(sums_ref)
     mask = all_ref[MASK]
     beta = all_ref[BETA]
 
     @pl.loop(0, LEV)
     def _(level):
+        each(level)
         upper = jnp.minimum(level + 1, LEV - 1)
         u, v = all_ref[level], all_ref[LEV + level]
         grad_xx = 0.5 * (next_row(u) - last_row(u))
@@ -571,7 +467,7 @@
     return a0, a1, c, rr1, along
 
 
-def middle_kernel(total_ref, all_ref, r0_ref, v1_ref, v2_ref, gx_ref, gy_ref, gz_ref, s_ref, part_ref, r2_ref, q1_ref, sums_ref):
+def middle(total_ref, all_ref, r0_ref, v1_ref, v2_ref, gx_ref, gy_ref, gz_ref, s_ref, part_ref, r2_ref, q1_ref, sums_ref):
     a0, a1, c, _, _ = first_scalars(total_ref)
     sums_ref[...] = jnp.zeros_like(sums_ref)
     mask = all_ref[MASK]
@@ -616,7 +512,7 @@
     part_ref[...] = tile_of([(d[0], d[1]), (d[2], d[3]), (d[4], d[5]), (d[6], d[7]), (d[8], d[8])])
 
 
-def end_kernel(first_ref, second_ref, all_ref, r0_ref, v1_ref, v2_ref, s_ref, velocity_ref, spread_ref):
+def end(first_ref, second_ref, all_ref, r0_ref, v1_ref, v2_ref, s_ref, velocity_ref):
     a0, a1, c, rr1, pq = first_scalars(first_ref)
     pair = lambda i: (second_ref[i : i + 1, 0:1], second_ref[i : i + 1, 64:65])
     (rr2, rq), (qq, rs), (ss, sq), (tq, su), (uq, _) = (pair(i) for i in range(5))
@@ -655,46 +551,217 @@
             mean = mean + value
         means.append(all_ref[THICK] * (mean * (1.0 / LEV)))
     spread = 0.5 * (next_row(means[0]) - last_row(means[0])) + 0.5 * (next_col(means[1]) - last_col(means[1]))
-    spread_ref[...] = spread[:ROWS, :COLS]
-
-
-def solve(padded, most):
-    block = jax.ShapeDtypeStruct((2 * LEV, TALL, LONG), F32)
-    tile = jax.ShapeDtypeStruct((8, 128), F32)
-    level = jax.ShapeDtypeStruct((LEV, TALL, LONG), F32)
-    room = pltpu.CompilerParams(vmem_limit_bytes=56 << 20)
-    r0, v1, v2, gx, gy, gz, part = pl.pallas_call(
-        begin_kernel,
-        name="begin",
-        out_shape=(block, block, block, level, level, jax.ShapeDtypeStruct((LEV + 1, TALL, LONG), F32), tile),
-        in_specs=[VM] * 2,
-        out_specs=(VM,) * 7,
-        scratch_shapes=[pltpu.VMEM((LEV, TALL, LONG), F32), pltpu.VMEM((4, 8, COLS), F32)],
-        compiler_params=room,
-    )(padded, most)
-    first = total(part, "total_first", 1)
-    s, part = pl.pallas_call(
-        middle_kernel,
-        name="middle",
-        out_shape=(block, tile),
-        in_specs=[VM] * 8,
-        out_specs=(VM,) * 2,
-        scratch_shapes=[pltpu.VMEM((2 * LEV, TALL, LONG), F32)] * 2 + [pltpu.VMEM((9, 8, COLS), F32)],
-        compiler_params=room,
-    )(first, padded, r0, v1, v2, gx, gy, gz)
-    second = total(part, "total_second", 6)
-    velocity, spread = pl.pallas_call(
-        end_kernel,
-        name="end",
-        out_shape=(
-            jax.ShapeDtypeStruct((2 * LEV, ROWS, COLS), F32),
-            jax.ShapeDtypeStruct((ROWS, COLS), F32),
+    return spread[:ROWS, :COLS]
+
+
+def joined(tiles):
+    row = lax.broadcasted_iota(jnp.int32, tiles.shape[1:], 0)
+    return jnp.where(row < 7, jnp.sum(tiles, axis=0), jnp.max(tiles, axis=0))
+
+
+class Total:
+    def __init__(self, part_ref, near_ref, half_ref, far_ref, sems):
+        y, x = lax.axis_index("ty"), lax.axis_index("tx")
+        tall, wide = lax.axis_size("ty"), lax.axis_size("tx")
+        core, chip = x % 2, x // 2
+        near, far = tall * 2, wide // 2
+        self.me, self.chip = y * 2 + core, chip
+        ids = [(self.me + i) % near for i in range(1, near)]
+        self.near_devices = [(i // 2, chip * 2 + i % 2) for i in ids]
+        self.far_devices = [(y, ((chip + i) % far) * 2 + core) for i in range(1, far)]
+        self.part, self.near, self.half, self.far, self.sems = part_ref, near_ref, half_ref, far_ref, sems
+
+    def send(self, source, target, place, devices, first):
+        for device in devices:
+            pltpu.make_async_remote_copy(
+                source, target.at[place], self.sems.at[first], self.sems.at[first + 1],
+                device_id=device, device_id_type=MESH,
+            ).start()
+        target[pl.ds(place, 1)] = source[...][None]
+
+    def wait(self, target, devices, first):
+        whole = pl.ds(0, len(devices))
+        pltpu.make_async_remote_copy(
+            target.at[whole], target.at[whole], self.sems.at[first], self.sems.at[first + 1],
+            device_id=devices[0], device_id_type=MESH,
+        ).wait()
+
+    def start(self):
+        self.send(self.part, self.near, self.me, self.near_devices, 0)
+
+    def turn(self):
+        self.wait(self.near, self.near_devices, 0)
+        self.half[...] = joined(self.near[...])
+        self.send(self.half, self.far, self.chip, self.far_devices, 2)
+
+    def finish(self, sum_ref):
+        self.wait(self.far, self.far_devices, 2)
+        sum_ref[...] = joined(self.far[...])
+
+
+def send_block(source, target, peer, me, sems):
+    pltpu.make_async_remote_copy(
+        source.at[peer], target.at[me], sems.at[0], sems.at[1], device_id=at(peer), device_id_type=MESH
+    ).start()
+
+
+def await_blocks(source, target, me, peers, sems):
+    target[pl.ds(me, 1)] = source[pl.ds(me, 1)]
+    others = pl.ds(0, peers - 1)
+    pltpu.make_async_remote_copy(
+        source.at[others], target.at[others], sems.at[0], sems.at[1],
+        device_id=at((me + 1) % peers), device_id_type=MESH,
+    ).wait()
+
+
+def send_group(source, target, g, me, sems):
+    for s in range(GROUP):
+        peer = g * GROUP + s
+
+        @pl.when(peer != me)
+        def _():
+            send_block(source, target, peer, me, sems)
+
+
+def whole_kernel(
+    vel_ref, stiff_ref, mask_ref, thick_ref, bed_ref, beta_ref, table_ref, cols_ref, class_ref, weights_ref,
+    velocity_ref, surface_ref, land_ref, spread_ref, first_ref,
+    all_ref, left_ref, right_ref, from_right, from_left,
+    send_ref, cell_ref, most_ref, route_left, route_right, route_total,
+    got_ref, found_ref, back_ref, value_ref, last_ref,
+    r0_ref, v1_ref, v2_ref, r2_ref, q1_ref, s_ref, gx_ref, gy_ref, gz_ref, mu_ref,
+    sums_ref, part1_ref, near1_ref, half1_ref, far1_ref, part2_ref, near2_ref, half2_ref, far2_ref, second_ref,
+    terms_ref, surface_terms, denom_ref, smb_ref, numer_ref,
+    halo_out, halo_in, total1_sem, total2_sem, to_owner, from_owner, to_land,
+):
+    me, peers = place()
+    groups = peers // GROUP
+    barrier = pltpu.get_barrier_semaphore()
+
+    def greet(p):
+        for step in range(4 * p + 1, min(4 * p + 5, 128)):
+            pl.semaphore_signal(barrier, inc=1, device_id=at((me + step) % peers), device_id_type=MESH)
+
+    pack_halo((vel_ref, stiff_ref, mask_ref, thick_ref, bed_ref, beta_ref), all_ref, left_ref, right_ref, greet)
+    pl.semaphore_wait(barrier, peers - 1)
+    halo = halo_copies(all_ref, left_ref, right_ref, from_right, from_left, halo_out, halo_in)
+    for copy in halo:
+        copy.start()
+    route_kernel(
+        peers, None, cols_ref, class_ref, weights_ref, send_ref, cell_ref, most_ref, route_left, route_right, route_total
+    )
+    for copy in halo:
+        copy.wait()
+    unpack_halo(all_ref, from_right, from_left)
+
+    def to_owners(level):
+        for i in range(13):
+            step = level * 13 + i + 1
+
+            @pl.when(step < peers)
+            def _():
+                send_block(send_ref, got_ref, (me + step) % peers, me, to_owner)
+
+    begin(to_owners, all_ref, most_ref, r0_ref, v1_ref, v2_ref, gx_ref, gy_ref, gz_ref, part1_ref, mu_ref, sums_ref)
+    total1 = Total(part1_ref, near1_ref, half1_ref, far1_ref, total1_sem)
+    total1.start()
+    await_blocks(send_ref, got_ref, me, peers, to_owner)
+    terms_ref[...] = table_terms(table_ref[...])
+    denom_ref[...] = jnp.zeros_like(denom_ref)
+
+    def own_group(g):
+        @pl.when(g > 0)
+        def _():
+            send_group(found_ref, back_ref, g - 1, me, from_owner)
+
+        owner_group(g, got_ref, terms_ref, denom_ref, found_ref)
+
+    pl.loop(0, groups // 2)(own_group)
+    total1.turn()
+    pl.loop(groups // 2, groups)(own_group)
+    total1.finish(first_ref)
+    send_group(found_ref, back_ref, groups - 1, me, from_owner)
+    middle(first_ref, all_ref, r0_ref, v1_ref, v2_ref, gx_ref, gy_ref, gz_ref, s_ref, part2_ref, r2_ref, q1_ref, sums_ref)
+    total2 = Total(part2_ref, near2_ref, half2_ref, far2_ref, total2_sem)
+    total2.start()
+    await_blocks(found_ref, back_ref, me, peers, from_owner)
+    smb_ref[...] = jnp.zeros_like(smb_ref)
+
+    def cell_group(g):
+        scatter_group(g, cell_ref, send_ref, back_ref, smb_ref)
+
+    pl.loop(0, groups // 2)(cell_group)
+    total2.turn()
+    pl.loop(groups // 2, groups)(cell_group)
+    total2.finish(second_ref)
+    spread = end(first_ref, second_ref, all_ref, r0_ref, v1_ref, v2_ref, s_ref, velocity_ref)
+    spread_ref[...] = spread
+    smb = smb_ref[:HIGH, :] + smb_ref[HIGH:, :]
+    halves = []
+    for h in range(2):
+        side = slice(h * 128, (h + 1) * 128)
+        half = bed_ref[:, side] + thick_ref[:, side] + 0.5 * (smb[h * ROWS : (h + 1) * ROWS] - spread[:, side])
+        surface_ref[:, side] = half
+        halves.append(half)
+    surface_terms[...] = table_terms(jnp.concatenate(halves, axis=0))
+
+    @pl.loop(0, groups)
+    def _(g):
+        @pl.when(g > 0)
+        def _():
+            send_group(value_ref, last_ref, g - 1, me, to_land)
+
+        gather_group(g, surface_terms, cell_ref, value_ref)
+
+    numer_ref[...] = jnp.zeros_like(numer_ref)
+    send_group(value_ref, last_ref, groups - 1, me, to_land)
+    await_blocks(value_ref, last_ref, me, peers, to_land)
+
+    @pl.loop(0, groups)
+    def _(g):
+        scatter_group(g, got_ref, got_ref, last_ref, numer_ref)
+
+    used = land_ref.shape[0]
+    numer = numer_ref[:used, :] + numer_ref[HIGH : HIGH + used, :]
+    denom = denom_ref[:used, :] + denom_ref[HIGH : HIGH + used, :]
+    land_ref[...] = numer / (denom + 1.0)
+
+
+def whole(velocity, stiffness, mask, thickness, bed, beta, table, cols, kind, weights):
+    tall, wide = lax.axis_size("ty"), lax.axis_size("tx")
+    peers = tall * wide
+    shape = lambda *dims: jax.ShapeDtypeStruct(dims, F32)
+    room = lambda *dims: pltpu.VMEM(dims, F32)
+    block, level = (2 * LEV, TALL, LONG), (LEV, TALL, LONG)
+    sum_room = [room(8, 128), room(2 * tall, 8, 128), room(8, 128), room(wide // 2, 8, 128)]
+    pair = pltpu.SemaphoreType.DMA((2,))
+    return pl.pallas_call(
+        whole_kernel,
+        name="whole",
+        out_shape=(shape(2 * LEV, ROWS, COLS), shape(ROWS, COLS), shape(*table.shape), shape(ROWS, COLS), shape(8, 128)),
+        in_specs=[VM] * 10,
+        out_specs=(VM,) * 5,
+        scratch_shapes=[
+            room(PLANES, TALL, LONG), room(PACKS, ROWS, 128), room(PACKS, ROWS, 128),
+            room(PACKS, TALL, 128), room(PACKS, TALL, 128),
+            room(peers, 8, SLOTS), room(peers, 4, SLOTS), room(8, 128),
+            pltpu.VMEM((6 * peers, 8 * COLS), BF), pltpu.VMEM((SLOTS, 8 * COLS), BF), room(6 * peers, SLOTS),
+            room(peers, 8, SLOTS), room(peers, 4, SLOTS), room(peers, 4, SLOTS), room(peers, 4, SLOTS), room(peers, 4, SLOTS),
+            room(*block), room(*block), room(*block), room(*block), room(*block), room(*block),
+            room(*level), room(*level), room(LEV + 1, TALL, LONG), room(*level),
+            room(9, 8, COLS), *sum_room, *sum_room, room(8, 128),
+            pltpu.VMEM((128, 3 * HIGH), BF), pltpu.VMEM((128, 3 * HIGH), BF),
+            room(2 * HIGH, 128), room(2 * HIGH, 128), room(2 * HIGH, 128),
+            pltpu.SemaphoreType.DMA((8,)), pltpu.SemaphoreType.DMA((8,)),
+            pltpu.SemaphoreType.DMA((4,)), pltpu.SemaphoreType.DMA((4,)), pair, pair, pair,
+        ],
+        compiler_params=pltpu.CompilerParams(
+            collective_id=1, has_side_effects=True, vmem_limit_bytes=60 << 20
         ),
-        in_specs=[VM] * 7,
-        out_specs=(VM,) * 2,
-        compiler_params=room,
-    )(first, second, padded, r0, v1, v2, s)
-    return velocity.reshape(2, LEV, ROWS, COLS), spread, first[7, 0]
+    )(
+        velocity.reshape(2 * LEV, ROWS, COLS), stiffness, mask, thickness, bed, beta, table,
+        cols.reshape(4 * ROWS, COLS), kind, weights.reshape(4 * ROWS, COLS),
+    )
 
 
 def on_device(
@@ -709,53 +776,50 @@
     correlation_cols,
     correlation_weights,
 ):
-    rows, cols = bed.shape
-    own_table = land_smb.reshape(-1, 128)
+    table = land_smb.reshape(-1, 128)
+    velocity, surface, land, spread, first = whole(
+        velocity_start, stiffness, ice_mask, thickness, bed, beta, table, correlation_cols, elev_class, correlation_weights
+    )
+    turns = ((first[7, 0].astype(jnp.int32) + SLOTS - 1) // SLOTS).astype(jnp.int32)
+
+    def swap(array):
+        return lax.all_to_all(array, ("ty", "tx"), 0, 0, tiled=True)
 
     def turn(number):
         return route(
             jnp.full((1,), number, jnp.int32), correlation_cols, elev_class, correlation_weights
         )
 
-    def balance_and_weights(send, cell, got, swap):
-        denom, found = owner(own_table, got)
-        return scatter(cell, send, swap(found)), denom
-
-    def plain_swap(array):
-        return lax.all_to_all(array, ("ty", "tx"), 0, 0, tiled=True)
-
-    send, cell, most = turn(0)
-    got = exchange(send, "to_owner", 2)
-    smb_ice, denom = balance_and_weights(send, cell, got, lambda a: exchange(a, "from_owner", 3))
-
-    padded = with_halo(velocity_start, stiffness, ice_mask, thickness, bed, beta)
-    velocity, spread, most = solve(padded, most)
-    turns = ((most.astype(jnp.int32) + SLOTS - 1) // SLOTS).astype(jnp.int32)
-
-    def more_balance(carry):
-        number, smb, weights = carry
-        send, cell, _ = turn(number)
-        add_smb, add_weights = balance_and_weights(send, cell, plain_swap(send), plain_swap)
-        return number + 1, smb + add_smb, weights + add_weights
-
     def unfinished(carry):
         return carry[0] < turns
 
-    _, smb_ice, denom = lax.while_loop(unfinished, more_balance, (jnp.int32(1), smb_ice, denom))
-    surface = bed + thickness + 0.5 * (smb_ice.reshape(rows, cols) - spread)
-    surface_rows = surface.reshape(-1, 128)
-    numer = scatter(got, got, exchange(gather(surface_rows, cell), "to_land", 4))
-
-    def more_numer(carry):
-        number, numer = carry
-        send, cell, _ = turn(number)
-        got = plain_swap(send)
-        return number + 1, numer + scatter(got, got, plain_swap(gather(surface_rows, cell)))
-
-    _, numer = lax.while_loop(unfinished, more_numer, (jnp.int32(1), numer))
-    used = own_table.shape[0]
-    land_surface = (numer[:used] / (denom[:used] + 1.0)).reshape(land_smb.shape)
-    return (velocity, surface, land_surface)
+    def in_turns():
+        def balance(carry):
+            number, smb, denom = carry
+            send, cell, _ = turn(number)
+            add_denom, found = owner(table, swap(send))
+            return number + 1, smb + scatter(cell, send, swap(found)), denom + add_denom
+
+        none = jnp.zeros((HIGH, 128), F32)
+        _, smb, denom = lax.while_loop(unfinished, balance, (jnp.int32(0), none, none))
+        halves = [
+            bed[:, s] + thickness[:, s] + 0.5 * (smb[h * ROWS : (h + 1) * ROWS] - spread[:, s])
+            for h, s in enumerate((slice(0, 128), slice(128, 256)))
+        ]
+        rows = jnp.concatenate(halves, axis=0)
+
+        def raised(carry):
+            number, numer = carry
+            send, cell, _ = turn(number)
+            got = swap(send)
+            return number + 1, numer + scatter(got, got, swap(gather(rows, cell)))
+
+        _, numer = lax.while_loop(unfinished, raised, (jnp.int32(0), none))
+        used = table.shape[0]
+        return jnp.concatenate(halves, axis=1), numer[:used] / (denom[:used] + 1.0)
+
+    surface, land = lax.cond(turns > 1, in_turns, lambda: (surface, land))
+    return velocity.reshape(velocity_start.shape), surface, land.reshape(land_smb.shape)
 
 
 def solution(mesh):

time: 213 us -> 124 us (0.58)
  Pallas kernels: 200 us -> 117 us
  local copies, waits for them, and re-layouts: 8.13 us -> 4.24 us
    pallas_call x14 -> x1, Pallas kernels: 200 us -> 117 us  [whole(): pl.pallas_call(whole_kernel, name='whole', out_shape=(shape(2 * LEV, ROWS...]
    unnamed x34 -> x14, local copies, waits for them, and re-layouts: 6.29 us -> 1.66 us
where the time goes in v1:
time: 124 us; the launch traced here: 123 us
  Pallas kernels  117 us (94%)
  local copies, waits for them, and re-layouts  4.24 us (3%)
  between operations  1.4 us (1%)
    pallas_call x1, Pallas kernels, whole(): pl.pallas_call(whole_kernel, name='whole', out_shape=(shape(2 * LEV, ROWS...  117 us

profile of v1, /device:TPU:25, one launch (start us, length us, event | category | flops | bytes accessed | tf_op | source)
XLA Modules:
  0.0 123.4 jit_solution(11334824251782209877)
XLA Ops:
  0.6 0.0 copy-start.2
  0.6 0.8 reshape.46.table_ref
  1.4 0.0 copy-done.2
  1.4 0.0 copy-start
  1.4 0.0 copy-start.1
  1.4 0.0 copy-start.5
  1.4 117.5 %whole.1 = (f32[20,32,256]{2,1,0:T(8,128)}, f32[32,256]{1,0:T(8,128)S(1)}, f32[40,128]{1,0:T(8,128)S(1)}, f32[32,256]{1,0:T(8,128)S(1)}, f32[8,128]{1,0:T(8,128)}) custom-call(f32[20,32,256]{2,1,0:T(8,128)} %bitcast.29, f32[10,32,256]{2,1,0:T(8,128)} %stiff_ref.1, s32[32,256]{1,0:T(8,128)} %mask_ref.1, f32[32,256]{1,0:T(8,128)} %thick_ref.1, ...), custom_call_target="tpu_custom_call" | custom-call | tf_op jit(solution)/shard_map/whole/pallas_call | solution.py:738
  118.9 0.0 copy-start.4
  118.9 1.2 slice.33
  120.8 0.0 copy-done
  120.8 0.0 copy-done.1
  120.8 0.0 copy-done.5
  120.8 0.0 copy-done.4
  120.8 0.0 copy-start.3
  120.9 0.3 conditional.1
  121.1 0.6 reshape.53
  121.7 0.2 copy-done.3
  121.9 0.8 copy.36
  122.8 0.6 copy.37
Async XLA Ops:
  0.6 0.8 copy-start.2
  1.4 119.4 %copy-start = (s32[4,32,256]{2,1,0:T(8,128)S(1)}, s32[4,32,256]{2,1,0:T(8,128)}, u32[]{:S(2)}) copy-start(s32[4,32,256]{2,1,0:T(8,128)} %param.24) | copy-start | bytes 393220
  1.4 119.4 %copy-start.1 = (f32[4,32,256]{2,1,0:T(8,128)S(1)}, f32[4,32,256]{2,1,0:T(8,128)}, u32[]{:S(2)}) copy-start(f32[4,32,256]{2,1,0:T(8,128)} %param.25) | copy-start | bytes 393220
  1.4 119.4 %copy-start.5 = (f32[32,256]{1,0:T(8,128)S(1)}, f32[32,256]{1,0:T(8,128)}, u32[]{:S(2)}) copy-start(f32[32,256]{1,0:T(8,128)} %bed_ref.1) | copy-start | bytes 98308
  118.9 1.9 %copy-start.4 = (f32[32,256]{1,0:T(8,128)S(1)}, f32[32,256]{1,0:T(8,128)}, u32[]{:S(2)}) copy-start(f32[32,256]{1,0:T(8,128)} %thick_ref.1) | copy-start | bytes 98308
  120.8 1.1 copy-start.3

commit v2 on v1

--- a/solution.py
+++ b/solution.py
@@ -30,18 +30,19 @@
 
 
 def hot(size, row):
-    return jnp.where(is_row(size, row), 1.0, 0.0).astype(BF)
-
-
-def route_kernel(peers, turn_ref, cols_ref, class_ref, weights_ref, send_ref, cell_ref, most_ref, left_ref, right_ref, total_ref):
+    rows = lax.broadcasted_iota(jnp.int32, (size, row.shape[1]), 0).astype(F32).astype(BF)
+    return jnp.where(rows == row.astype(F32).astype(BF), jnp.ones((), BF), jnp.zeros((), BF))
+
+
+def route_kernel(peers, turn_ref, cols_ref, class_ref, weights_ref, send_ref, cell_ref, most_ref, left_ref, right_ref, total_ref, stack_ref, counts_ref):
     width = cols_ref.shape[1]
-    step = 8
-    before = lax.broadcasted_iota(jnp.int32, (width, 2 * width), 0) < lax.broadcasted_iota(
-        jnp.int32, (width, 2 * width), 1
+    step, half = 8, peers // 2
+    before = lax.broadcasted_iota(jnp.int32, (width, width), 0) < lax.broadcasted_iota(
+        jnp.int32, (width, width), 1
     )
     ahead = jnp.where(before, 1.0, 0.0).astype(BF)
     first = 0 if turn_ref is None else turn_ref[0] * SLOTS
-    most = jnp.zeros((peers, width), F32)
+    most = jnp.zeros((peers, 128), F32)
     for k in range(4):
         total_ref[...] = jnp.zeros_like(total_ref)
 
@@ -52,27 +53,37 @@
             dest = cols >> 9
             lane = lax.broadcasted_iota(jnp.int32, cols.shape, 1)
             row = lax.broadcasted_iota(jnp.int32, cols.shape, 0) + g * step
-            whole = (kind * 4 + ((cols >> 7) & 3), cols & 127, (lane >> 7) * 32 + row, lane & 127)
+            whole = (((cols >> 7) & 3) * 10 + kind, cols & 127, (lane >> 7) * 32 + row, lane & 127)
             fields = [v.astype(F32) for v in whole]
             w = weights_ref[pl.ds(at, step), :]
             w_top = w.astype(BF).astype(F32)
             fields += [w_top, w - w_top]
             for r in range(step):
-                one = slice(r, r + 1)
-                mask = is_row(peers, dest[one])
-                picked = jnp.where(mask, 1.0, 0.0).astype(BF)
-                counts = jnp.dot(picked, ahead, preferred_element_type=F32)
-                rank = jnp.sum(jnp.where(mask, counts[:, :width] + base, 0.0), axis=0, keepdims=True)
-                base = base + counts[:, width:]
-                span = pl.ds(r * width, width)
+                stack_ref[r * peers : (r + 1) * peers, :] = hot(peers, dest[r : r + 1])
+            counts_ref[...] = jnp.dot(stack_ref[...], ahead, preferred_element_type=F32)
+            for r in range(step):
+                one, span = slice(r, r + 1), pl.ds(r * width, width)
+                picked = stack_ref[r * peers : (r + 1) * peers, :]
+                counts = counts_ref[r * peers : (r + 1) * peers, :]
+                so_far = jnp.concatenate([base] * (width // 128), axis=1)
+                rank = jnp.sum(picked.astype(F32) * (counts + so_far), axis=0, keepdims=True)
+                last = counts[:, width - 1 :] + picked[:, width - 128 :].astype(F32)[:, 127:]
+                base = base + jnp.broadcast_to(last, (peers, 128))
+                slot = rank.astype(jnp.int32) - first
+                kept = (slot >= 0) & (slot < SLOTS)
+                slot = jnp.where(kept, slot + jnp.where(dest[one] < half, 0, SLOTS), -1)
+                right_ref[:, span] = hot(2 * SLOTS, slot)
+                folded_in = picked[:half] + picked[half:]
                 for f, value in enumerate(fields):
-                    left_ref[f * peers : (f + 1) * peers, span] = picked * value[one].astype(BF)
-                right_ref[:, span] = hot(SLOTS, rank.astype(jnp.int32) - first)
+                    left_ref[f * half : (f + 1) * half, span] = folded_in * value[one].astype(BF)
             total_ref[...] += lax.dot_general(left_ref[...], right_ref[...], NT, preferred_element_type=F32)
             return base
 
-        base = lax.fori_loop(0, 32 // step, body, jnp.zeros((peers, width), F32))
-        f = [total_ref[i * peers : (i + 1) * peers, :] for i in range(6)]
+        base = lax.fori_loop(0, 32 // step, body, jnp.zeros((peers, 128), F32))
+        f = [
+            jnp.concatenate([total_ref[i * half : (i + 1) * half, j * SLOTS : (j + 1) * SLOTS] for j in range(2)], axis=0)
+            for i in range(6)
+        ]
         send_ref[:, k, :] = f[0] * 128.0 + f[1]
         cell_ref[:, k, :] = f[2] * 128.0 + f[3]
         send_ref[:, 4 + k, :] = f[4] + f[5]
@@ -93,9 +104,11 @@
         in_specs=[SM, VM, VM, VM],
         out_specs=(VM, VM, VM),
         scratch_shapes=[
-            pltpu.VMEM((6 * peers, 8 * width), BF),
-            pltpu.VMEM((SLOTS, 8 * width), BF),
-            pltpu.VMEM((6 * peers, SLOTS), F32),
+            pltpu.VMEM((3 * peers, 8 * width), BF),
+            pltpu.VMEM((2 * SLOTS, 8 * width), BF),
+            pltpu.VMEM((3 * peers, 2 * SLOTS), F32),
+            pltpu.VMEM((8 * peers, width), BF),
+            pltpu.VMEM((8 * peers, width), F32),
         ],
         compiler_params=pltpu.CompilerParams(vmem_limit_bytes=48 << 20),
     )(turn, cols.reshape(rows, width), kind, weights.reshape(rows, width))
@@ -106,15 +119,21 @@
     return at >> 7, at & 127
 
 
-def table_terms(table):
-    padded = jnp.concatenate([table, jnp.zeros((HIGH - table.shape[0], 128), F32)], axis=0) if table.shape[0] < HIGH else table
-    return jnp.concatenate([p.astype(F32) for p in parts(padded, 3)], axis=0).T.astype(BF)
-
-
-def look_up(terms, high, low_masks):
-    stacked = jnp.concatenate([high] * 3, axis=0)
-    found = jnp.dot(terms, stacked, preferred_element_type=F32)
-    return jnp.sum(jnp.where(low_masks, found, 0.0), axis=0, keepdims=True)
+def table_terms(table, count):
+    return jnp.concatenate([p.astype(F32) for p in parts(table, count)], axis=0).T.astype(BF)
+
+
+def look_up(terms, rows, at):
+    high = hot(rows, at >> 7)
+    found = jnp.dot(terms, jnp.concatenate([high] * (terms.shape[1] // rows), axis=0), preferred_element_type=F32)
+    rows = 128
+    while rows > 8:
+        rows //= 2
+        upper = jnp.broadcast_to(at & rows, (8, at.shape[1])) > 0
+        found = jnp.concatenate(
+            [jnp.where(upper, found[rows + i : rows + i + 8], found[i : i + 8]) for i in range(0, rows, 8)], axis=0
+        )
+    return jnp.sum(jnp.where(is_row(8, at & 7), found, 0.0), axis=0, keepdims=True)
 
 
 def across(pieces):
@@ -126,24 +145,11 @@
     total_ref[...] += lax.dot_general(both, low, NT, preferred_element_type=F32)
 
 
-GROUP = 4
+GROUP = 16
 
 
 def flat_rows(tiles):
     return [tiles[s, k : k + 1, :] for s in range(tiles.shape[0]) for k in range(4)]
-
-
-def owner_group(g, got_ref, terms_ref, total_ref, back_ref):
-    tile = got_ref[pl.ds(g * GROUP, GROUP), :, :]
-    high, low = spots(tile[:, :4, :])
-    w = across(flat_rows(tile[:, 4:, :]))
-    high_hot = hot(HIGH, across(flat_rows(high)))
-    low_mask = is_row(128, across(flat_rows(low)))
-    low_hot = jnp.where(low_mask, 1.0, 0.0).astype(BF)
-    w_top = w.astype(BF).astype(F32)
-    add_in(total_ref, (w_top, w - w_top), high_hot, low_hot)
-    found = look_up(terms_ref[...], high_hot, low_mask)
-    put_rows(back_ref, g, found)
 
 
 def put_rows(out_ref, g, found):
@@ -153,29 +159,30 @@
             out_ref[g * GROUP + s, k : k + 1, :] = found[:, i * 128 : (i + 1) * 128]
 
 
+def owner_group(g, got_ref, terms_ref, total_ref, back_ref):
+    tile = got_ref[pl.ds(g * GROUP, GROUP), :, :]
+    at_all = across(flat_rows(tile[:, :4, :].astype(jnp.int32)))
+    w = across(flat_rows(tile[:, 4:, :]))
+    w_top = w.astype(BF).astype(F32)
+    add_in(total_ref, (w_top, w - w_top), hot(HIGH, at_all >> 7), hot(128, at_all & 127))
+    put_rows(back_ref, g, look_up(terms_ref[...], 40, at_all))
+
+
 def gather_group(g, terms_ref, where_ref, out_ref):
-    high, low = spots(where_ref[pl.ds(g * GROUP, GROUP), :, :])
-    found = look_up(
-        terms_ref[...], hot(HIGH, across(flat_rows(high))), is_row(128, across(flat_rows(low)))
-    )
-    put_rows(out_ref, g, found)
+    at_all = across(flat_rows(where_ref[pl.ds(g * GROUP, GROUP), :, :].astype(jnp.int32)))
+    put_rows(out_ref, g, look_up(terms_ref[...], HIGH, at_all))
 
 
 def scatter_group(g, where_ref, weights_ref, values_ref, total_ref):
     span = pl.ds(g * GROUP, GROUP)
-    high, low = spots(where_ref[span, :4, :])
+    at_all = across(flat_rows(where_ref[span, :4, :].astype(jnp.int32)))
     v = across(flat_rows(weights_ref[span, 4:, :] * values_ref[span, :, :]))
     v_top = v.astype(BF).astype(F32)
-    add_in(
-        total_ref,
-        (v_top, v - v_top),
-        hot(HIGH, across(flat_rows(high))),
-        hot(128, across(flat_rows(low))),
-    )
+    add_in(total_ref, (v_top, v - v_top), hot(HIGH, at_all >> 7), hot(128, at_all & 127))
 
 
 def owner_kernel(table_ref, got_ref, denom_ref, back_ref, terms_ref, total_ref):
-    terms_ref[...] = table_terms(table_ref[...])
+    terms_ref[...] = table_terms(table_ref[...], 3)
     total_ref[...] = jnp.zeros_like(total_ref)
 
     @pl.loop(0, got_ref.shape[0] // GROUP)
@@ -193,13 +200,13 @@
         out_shape=(jax.ShapeDtypeStruct((HIGH, 128), F32), jax.ShapeDtypeStruct((peers, 4, SLOTS), F32)),
         in_specs=[VM, VM],
         out_specs=(VM, VM),
-        scratch_shapes=[pltpu.VMEM((128, 3 * HIGH), BF), pltpu.VMEM((2 * HIGH, 128), F32)],
+        scratch_shapes=[pltpu.VMEM((128, 120), BF), pltpu.VMEM((2 * HIGH, 128), F32)],
         compiler_params=pltpu.CompilerParams(vmem_limit_bytes=48 << 20),
     )(table, got)
 
 
 def gather_kernel(table_ref, where_ref, out_ref, terms_ref):
-    terms_ref[...] = table_terms(table_ref[...])
+    terms_ref[...] = table_terms(table_ref[...], 2)
 
     @pl.loop(0, where_ref.shape[0] // GROUP)
     def _(g):
@@ -213,7 +220,7 @@
         out_shape=jax.ShapeDtypeStruct(where.shape, F32),
         in_specs=[VM, VM],
         out_specs=VM,
-        scratch_shapes=[pltpu.VMEM((128, 3 * HIGH), BF)],
+        scratch_shapes=[pltpu.VMEM((128, 128), BF)],
         compiler_params=pltpu.CompilerParams(vmem_limit_bytes=48 << 20),
     )(table, where)
 
@@ -248,6 +255,49 @@
 def at(peer):
     wide = lax.axis_size("tx")
     return (peer // wide, peer % wide)
+
+
+def meet(me, peers):
+    barrier = pltpu.get_barrier_semaphore()
+
+    @pl.loop(1, peers)
+    def _(step):
+        pl.semaphore_signal(barrier, inc=1, device_id=at((me + step) % peers), device_id_type=MESH)
+
+    pl.semaphore_wait(barrier, peers - 1)
+
+
+def exchange_kernel(send_ref, got_ref, out_sem, in_sem, own_sem):
+    me, peers = place()
+    own = pltpu.make_async_copy(send_ref.at[me], got_ref.at[me], own_sem)
+    own.start()
+    meet(me, peers)
+
+    @pl.loop(1, peers)
+    def _(step):
+        peer = (me + step) % peers
+        pltpu.make_async_remote_copy(
+            send_ref.at[peer], got_ref.at[me], out_sem, in_sem, device_id=at(peer), device_id_type=MESH
+        ).start()
+
+    own.wait()
+    others = pl.ds(0, peers - 1)
+    whole = pltpu.make_async_remote_copy(
+        send_ref.at[others], got_ref.at[others], out_sem, in_sem, device_id=at((me + 1) % peers), device_id_type=MESH
+    )
+    whole.wait()
+
+
+def exchange(send, name, number):
+    return pl.pallas_call(
+        exchange_kernel,
+        name=name,
+        out_shape=jax.ShapeDtypeStruct(send.shape, send.dtype),
+        in_specs=[VM],
+        out_specs=VM,
+        scratch_shapes=[pltpu.SemaphoreType.DMA] * 3,
+        compiler_params=pltpu.CompilerParams(collective_id=number, has_side_effects=True),
+    )(send)
 
 
 LEV = 10
@@ -625,9 +675,9 @@
 
 def whole_kernel(
     vel_ref, stiff_ref, mask_ref, thick_ref, bed_ref, beta_ref, table_ref, cols_ref, class_ref, weights_ref,
-    velocity_ref, surface_ref, land_ref, spread_ref, first_ref,
-    all_ref, left_ref, right_ref, from_right, from_left,
-    send_ref, cell_ref, most_ref, route_left, route_right, route_total,
+    velocity_ref, surface_ref, land_ref, spread_ref, fullest_ref,
+    first_ref, all_ref, left_ref, right_ref, from_right, from_left,
+    send_ref, cell_ref, most_ref, route_left, route_right, route_total, route_stack, route_counts,
     got_ref, found_ref, back_ref, value_ref, last_ref,
     r0_ref, v1_ref, v2_ref, r2_ref, q1_ref, s_ref, gx_ref, gy_ref, gz_ref, mu_ref,
     sums_ref, part1_ref, near1_ref, half1_ref, far1_ref, part2_ref, near2_ref, half2_ref, far2_ref, second_ref,
@@ -648,7 +698,8 @@
     for copy in halo:
         copy.start()
     route_kernel(
-        peers, None, cols_ref, class_ref, weights_ref, send_ref, cell_ref, most_ref, route_left, route_right, route_total
+        peers, None, cols_ref, class_ref, weights_ref, send_ref, cell_ref, most_ref, route_left, route_right, route_total,
+        route_stack, route_counts,
     )
     for copy in halo:
         copy.wait()
@@ -666,7 +717,8 @@
     total1 = Total(part1_ref, near1_ref, half1_ref, far1_ref, total1_sem)
     total1.start()
     await_blocks(send_ref, got_ref, me, peers, to_owner)
-    terms_ref[...] = table_terms(table_ref[...])
+    table = jnp.concatenate([table_ref[:, t * 128 : (t + 1) * 128] for t in range(4)], axis=0)
+    terms_ref[...] = table_terms(table, 3)
     denom_ref[...] = jnp.zeros_like(denom_ref)
 
     def own_group(g):
@@ -680,6 +732,7 @@
     total1.turn()
     pl.loop(groups // 2, groups)(own_group)
     total1.finish(first_ref)
+    fullest_ref[0, 0] = jnp.max(first_ref[7:8, :])
     send_group(found_ref, back_ref, groups - 1, me, from_owner)
     middle(first_ref, all_ref, r0_ref, v1_ref, v2_ref, gx_ref, gy_ref, gz_ref, s_ref, part2_ref, r2_ref, q1_ref, sums_ref)
     total2 = Total(part2_ref, near2_ref, half2_ref, far2_ref, total2_sem)
@@ -703,7 +756,7 @@
         half = bed_ref[:, side] + thick_ref[:, side] + 0.5 * (smb[h * ROWS : (h + 1) * ROWS] - spread[:, side])
         surface_ref[:, side] = half
         halves.append(half)
-    surface_terms[...] = table_terms(jnp.concatenate(halves, axis=0))
+    surface_terms[...] = table_terms(jnp.concatenate(halves, axis=0), 2)
 
     @pl.loop(0, groups)
     def _(g):
@@ -721,10 +774,13 @@
     def _(g):
         scatter_group(g, got_ref, got_ref, last_ref, numer_ref)
 
-    used = land_ref.shape[0]
-    numer = numer_ref[:used, :] + numer_ref[HIGH : HIGH + used, :]
-    denom = denom_ref[:used, :] + denom_ref[HIGH : HIGH + used, :]
-    land_ref[...] = numer / (denom + 1.0)
+    classes = land_ref.shape[0]
+    for t in range(4):
+        numer, denom = (
+            ref[t * classes : (t + 1) * classes, :] + ref[HIGH + t * classes : HIGH + (t + 1) * classes, :]
+            for ref in (numer_ref, denom_ref)
+        )
+        land_ref[:, t * 128 : (t + 1) * 128] = numer / (denom + 1.0)
 
 
 def whole(velocity, stiffness, mask, thickness, bed, beta, table, cols, kind, weights):
@@ -738,19 +794,21 @@
     return pl.pallas_call(
         whole_kernel,
         name="whole",
-        out_shape=(shape(2 * LEV, ROWS, COLS), shape(ROWS, COLS), shape(*table.shape), shape(ROWS, COLS), shape(8, 128)),
+        out_shape=(shape(2 * LEV, ROWS, COLS), shape(ROWS, COLS), shape(*table.shape), shape(ROWS, COLS), shape(1, 1)),
         in_specs=[VM] * 10,
-        out_specs=(VM,) * 5,
+        out_specs=(VM,) * 4 + (SM,),
         scratch_shapes=[
+            room(8, 128),
             room(PLANES, TALL, LONG), room(PACKS, ROWS, 128), room(PACKS, ROWS, 128),
             room(PACKS, TALL, 128), room(PACKS, TALL, 128),
             room(peers, 8, SLOTS), room(peers, 4, SLOTS), room(8, 128),
-            pltpu.VMEM((6 * peers, 8 * COLS), BF), pltpu.VMEM((SLOTS, 8 * COLS), BF), room(6 * peers, SLOTS),
+            pltpu.VMEM((3 * peers, 8 * COLS), BF), pltpu.VMEM((2 * SLOTS, 8 * COLS), BF), room(3 * peers, 2 * SLOTS),
+            pltpu.VMEM((8 * peers, COLS), BF), room(8 * peers, COLS),
             room(peers, 8, SLOTS), room(peers, 4, SLOTS), room(peers, 4, SLOTS), room(peers, 4, SLOTS), room(peers, 4, SLOTS),
             room(*block), room(*block), room(*block), room(*block), room(*block), room(*block),
             room(*level), room(*level), room(LEV + 1, TALL, LONG), room(*level),
             room(9, 8, COLS), *sum_room, *sum_room, room(8, 128),
-            pltpu.VMEM((128, 3 * HIGH), BF), pltpu.VMEM((128, 3 * HIGH), BF),
+            pltpu.VMEM((128, 120), BF), pltpu.VMEM((128, 128), BF),
             room(2 * HIGH, 128), room(2 * HIGH, 128), room(2 * HIGH, 128),
             pltpu.SemaphoreType.DMA((8,)), pltpu.SemaphoreType.DMA((8,)),
             pltpu.SemaphoreType.DMA((4,)), pltpu.SemaphoreType.DMA((4,)), pair, pair, pair,
@@ -776,14 +834,11 @@
     correlation_cols,
     correlation_weights,
 ):
-    table = land_smb.reshape(-1, 128)
-    velocity, surface, land, spread, first = whole(
-        velocity_start, stiffness, ice_mask, thickness, bed, beta, table, correlation_cols, elev_class, correlation_weights
+    velocity, surface, land, spread, fullest = whole(
+        velocity_start, stiffness, ice_mask, thickness, bed, beta, land_smb, correlation_cols, elev_class, correlation_weights
     )
-    turns = ((first[7, 0].astype(jnp.int32) + SLOTS - 1) // SLOTS).astype(jnp.int32)
-
-    def swap(array):
-        return lax.all_to_all(array, ("ty", "tx"), 0, 0, tiled=True)
+    turns = ((fullest[0, 0].astype(jnp.int32) + SLOTS - 1) // SLOTS).astype(jnp.int32)
+
 
     def turn(number):
         return route(
@@ -794,11 +849,13 @@
         return carry[0] < turns
 
     def in_turns():
+        table = jnp.concatenate([land_smb[:, t * 128 : (t + 1) * 128] for t in range(4)], axis=0)
+
         def balance(carry):
             number, smb, denom = carry
             send, cell, _ = turn(number)
-            add_denom, found = owner(table, swap(send))
-            return number + 1, smb + scatter(cell, send, swap(found)), denom + add_denom
+            add_denom, found = owner(table, exchange(send, "more_to_owner", 2))
+            return number + 1, smb + scatter(cell, send, exchange(found, "more_from_owner", 3)), denom + add_denom
 
         none = jnp.zeros((HIGH, 128), F32)
         _, smb, denom = lax.while_loop(unfinished, balance, (jnp.int32(0), none, none))
@@ -811,15 +868,16 @@
         def raised(carry):
             number, numer = carry
             send, cell, _ = turn(number)
-            got = swap(send)
-            return number + 1, numer + scatter(got, got, swap(gather(rows, cell)))
+            got = exchange(send, "again_to_owner", 4)
+            return number + 1, numer + scatter(got, got, exchange(gather(rows, cell), "again_to_land", 5))
 
         _, numer = lax.while_loop(unfinished, raised, (jnp.int32(0), none))
-        used = table.shape[0]
-        return jnp.concatenate(halves, axis=1), numer[:used] / (denom[:used] + 1.0)
+        ratio, classes = numer / (denom + 1.0), land_smb.shape[0]
+        land = jnp.concatenate([ratio[t * classes : (t + 1) * classes] for t in range(4)], axis=1)
+        return jnp.concatenate(halves, axis=1), land
 
     surface, land = lax.cond(turns > 1, in_turns, lambda: (surface, land))
-    return velocity.reshape(velocity_start.shape), surface, land.reshape(land_smb.shape)
+    return velocity.reshape(velocity_start.shape), surface, land
 
 
 def solution(mesh):

time: 124 us -> 94.8 us (0.76)
  Pallas kernels: 117 us -> 89.9 us
    pallas_call x1, Pallas kernels: 117 us -> 89.9 us  [whole(): pl.pallas_call(whole_kernel, name='whole', out_shape=(shape(2 * LEV, ROWS...]
    unnamed x14 -> x17, local copies, waits for them, and re-layouts: 1.66 us -> 3.09 us
    reshape x2 -> x0, local copies, waits for them, and re-layouts: 1.39 us -> none  [the longest x1 0.77 us: on_device(): table = land_smb.reshape(-1, 128)]
where the time goes in v2:
time: 94.8 us; the launch traced here: 94.5 us
  Pallas kernels  89.9 us (95%)
  local copies, waits for them, and re-layouts  3.09 us (3%)
  between operations  1.34 us (1%)
    pallas_call x1, Pallas kernels, whole(): pl.pallas_call(whole_kernel, name='whole', out_shape=(shape(2 * LEV, ROWS...  89.9 us
    unnamed x17, local copies, waits for them, and re-layouts  3.09 us

profile of v2, /device:TPU:25, one launch (start us, length us, event | category | flops | bytes accessed | tf_op | source)
XLA Modules:
  0.0 94.5 jit_solution(10339071500596370862)
XLA Ops:
  0.6 0.0 copy-start.9
  0.6 0.0 copy-start.10
  0.7 0.0 copy-start.13
  0.7 0.0 copy-start.14
  0.7 0.0 copy-start.15
  0.7 89.9 %whole.1 = (f32[20,32,256]{2,1,0:T(8,128)}, f32[32,256]{1,0:T(8,128)S(1)}, f32[10,512]{1,0:T(8,128)S(1)}, f32[32,256]{1,0:T(8,128)S(1)}, f32[1,1]{1,0:T(1,128)}) custom-call(f32[20,32,256]{2,1,0:T(8,128)} %bitcast.29, f32[10,32,256]{2,1,0:T(8,128)} %stiff_ref.1, s32[32,256]{1,0:T(8,128)} %mask_ref.1, f32[32,256]{1,0:T(8,128)} %thick_ref.1, ...), custom_call_target="tpu_custom_call" | custom-call | tf_op jit(solution)/shard_map/whole/pallas_call | solution.py:794
  90.6 0.0 copy-start.11
  91.2 0.0 copy-done.9
  91.2 0.0 copy-done.10
  91.2 0.0 copy-done.13
  91.2 0.0 copy-done.14
  91.3 0.0 copy-done.15
  91.3 0.1 copy-done.11
  91.4 0.0 copy-start.12
  91.4 0.2 conditional.1
  91.6 0.9 copy-done.12
  92.5 0.8 copy.37
  93.3 0.6 copy.38
  93.9 0.6 copy.39
Async XLA Ops:
  0.6 90.6 %copy-start.9 = (s32[4,32,256]{2,1,0:T(8,128)S(1)}, s32[4,32,256]{2,1,0:T(8,128)}, u32[]{:S(2)}) copy-start(s32[4,32,256]{2,1,0:T(8,128)} %param.24) | copy-start | bytes 393220
  0.6 90.6 %copy-start.10 = (f32[4,32,256]{2,1,0:T(8,128)S(1)}, f32[4,32,256]{2,1,0:T(8,128)}, u32[]{:S(2)}) copy-start(f32[4,32,256]{2,1,0:T(8,128)} %param.25) | copy-start | bytes 393220
  0.7 90.6 %copy-start.13 = (f32[32,256]{1,0:T(8,128)S(1)}, f32[32,256]{1,0:T(8,128)}, u32[]{:S(2)}) copy-start(f32[32,256]{1,0:T(8,128)} %thick_ref.1) | copy-start | bytes 98308
  0.7 90.6 %copy-start.14 = (f32[32,256]{1,0:T(8,128)S(1)}, f32[32,256]{1,0:T(8,128)}, u32[]{:S(2)}) copy-start(f32[32,256]{1,0:T(8,128)} %bed_ref.1) | copy-start | bytes 98308
  0.7 90.6 %copy-start.15 = (f32[10,512]{1,0:T(8,128)S(1)}, f32[10,512]{1,0:T(8,128)}, u32[]{:S(2)}) copy-start(f32[10,512]{1,0:T(8,128)} %table_ref.1) | copy-start | bytes 61444
  90.6 0.8 copy-start.11
  91.4 1.1 %copy-start.12 = (f32[20,32,256]{2,1,0:T(8,128)S(1)}, f32[20,32,256]{2,1,0:T(8,128)}, u32[]{:S(2)}) copy-start(f32[20,32,256]{2,1,0:T(8,128)} %get-tuple-element.126) | copy-start | bytes 1966084

commit v3 on v2

--- a/solution.py
+++ b/solution.py
@@ -848,35 +848,35 @@
     def unfinished(carry):
         return carry[0] < turns
 
-    def in_turns():
-        table = jnp.concatenate([land_smb[:, t * 128 : (t + 1) * 128] for t in range(4)], axis=0)
-
-        def balance(carry):
-            number, smb, denom = carry
-            send, cell, _ = turn(number)
-            add_denom, found = owner(table, exchange(send, "more_to_owner", 2))
-            return number + 1, smb + scatter(cell, send, exchange(found, "more_from_owner", 3)), denom + add_denom
-
-        none = jnp.zeros((HIGH, 128), F32)
-        _, smb, denom = lax.while_loop(unfinished, balance, (jnp.int32(0), none, none))
-        halves = [
-            bed[:, s] + thickness[:, s] + 0.5 * (smb[h * ROWS : (h + 1) * ROWS] - spread[:, s])
-            for h, s in enumerate((slice(0, 128), slice(128, 256)))
-        ]
-        rows = jnp.concatenate(halves, axis=0)
-
-        def raised(carry):
-            number, numer = carry
-            send, cell, _ = turn(number)
-            got = exchange(send, "again_to_owner", 4)
-            return number + 1, numer + scatter(got, got, exchange(gather(rows, cell), "again_to_land", 5))
-
-        _, numer = lax.while_loop(unfinished, raised, (jnp.int32(0), none))
-        ratio, classes = numer / (denom + 1.0), land_smb.shape[0]
-        land = jnp.concatenate([ratio[t * classes : (t + 1) * classes] for t in range(4)], axis=1)
-        return jnp.concatenate(halves, axis=1), land
-
-    surface, land = lax.cond(turns > 1, in_turns, lambda: (surface, land))
+    table = jnp.concatenate([land_smb[:, t * 128 : (t + 1) * 128] for t in range(4)], axis=0)
+    again = turns > 1
+    start = jnp.where(again, 0, turns)
+
+    def balance(carry):
+        number, smb, denom = carry
+        send, cell, _ = turn(number)
+        add_denom, found = owner(table, exchange(send, "more_to_owner", 2))
+        return number + 1, smb + scatter(cell, send, exchange(found, "more_from_owner", 3)), denom + add_denom
+
+    none = jnp.zeros((HIGH, 128), F32)
+    _, smb, denom = lax.while_loop(unfinished, balance, (start, none, none))
+    halves = [
+        bed[:, s] + thickness[:, s] + 0.5 * (smb[h * ROWS : (h + 1) * ROWS] - spread[:, s])
+        for h, s in enumerate((slice(0, 128), slice(128, 256)))
+    ]
+    rows = jnp.concatenate(halves, axis=0)
+
+    def raised(carry):
+        number, numer = carry
+        send, cell, _ = turn(number)
+        got = exchange(send, "again_to_owner", 4)
+        return number + 1, numer + scatter(got, got, exchange(gather(rows, cell), "again_to_land", 5))
+
+    _, numer = lax.while_loop(unfinished, raised, (start, none))
+    ratio, classes = numer / (denom + 1.0), land_smb.shape[0]
+    land_again = jnp.concatenate([ratio[t * classes : (t + 1) * classes] for t in range(4)], axis=1)
+    surface = jnp.where(again, jnp.concatenate(halves, axis=1), surface)
+    land = jnp.where(again, land_again, land)
     return velocity.reshape(velocity_start.shape), surface, land
 
 

time: 94.8 us -> 97.7 us (1.031)
  other arithmetic: 0 us -> 1.28 us
    select_n x0 -> x2, other arithmetic: none -> 1.24 us  [the longest x1 0.62 us: on_device(): land = jnp.where(again, land_again, land)]
    unnamed x17 -> x21, local copies, waits for them, and re-layouts: 3.09 us -> 3.85 us
where the time goes in v3:
time: 97.7 us; the launch traced here: 97.3 us
  Pallas kernels  90.4 us (93%)
  local copies, waits for them, and re-layouts  3.88 us (4%)
  between operations  1.46 us (1%)
  other arithmetic  1.28 us (1%)
    pallas_call x1, Pallas kernels, whole(): pl.pallas_call(whole_kernel, name='whole', out_shape=(shape(2 * LEV, ROWS...  90.4 us
    unnamed x21, local copies, waits for them, and re-layouts  3.85 us

profile of v3, /device:TPU:25, one launch (start us, length us, event | category | flops | bytes accessed | tf_op | source)
XLA Modules:
  0.0 97.3 jit_solution(4617518548189648824)
XLA Ops:
  0.6 0.0 copy-start.15
  0.6 0.0 copy-start.10
  0.7 90.4 %whole.1 = (f32[20,32,256]{2,1,0:T(8,128)}, f32[32,256]{1,0:T(8,128)}, f32[10,512]{1,0:T(8,128)}, f32[32,256]{1,0:T(8,128)}, f32[1,1]{1,0:T(1,128)}) custom-call(f32[20,32,256]{2,1,0:T(8,128)} %bitcast.29, f32[10,32,256]{2,1,0:T(8,128)} %stiff_ref.1, s32[32,256]{1,0:T(8,128)} %mask_ref.1, f32[32,256]{1,0:T(8,128)} %thick_ref.1, f32[32,256]{1,0:T(8,128)} %bed_ref.1, ...), custom_call_target="tpu_custom_call" | custom-call | tf_op jit(solution)/shard_map/whole/pallas_call | solution.py:794
  91.1 0.0 copy-start.9
  91.8 0.0 copy-done.15
  91.9 0.0 copy-start.11
  91.9 0.0 copy-done.10
  91.9 0.1 copy-done.9
  92.0 0.6 copy-done.11
  92.6 0.0 copy-start.13
  92.6 0.0 copy-start.14
  92.6 0.0 copy-start.18
  92.6 0.8 copy-done.13
  93.4 0.0 copy-done.14
  93.4 0.0 copy-done.18
  93.4 0.0 copy-start.17
  93.4 0.7 copy-done.17
  94.2 0.6 maximum_select_fusion
  94.8 0.0 copy-start.12
  94.8 0.3 while.23
  95.1 0.0 copy-start.16
  95.1 0.7 copy-done.16
  95.9 0.6 maximum_select_fusion.1
  96.5 0.0 copy-done.12
  96.5 0.8 copy.29
  (10 shorter events, 0.1 us)
Async XLA Ops:
  0.6 91.2 %copy-start.15 = (f32[10,512]{1,0:T(8,128)S(1)}, f32[10,512]{1,0:T(8,128)}, u32[]{:S(2)}) copy-start(f32[10,512]{1,0:T(8,128)} %table_ref.1) | copy-start | bytes 61444
  0.6 91.2 %copy-start.10 = (f32[4,32,256]{2,1,0:T(8,128)S(1)}, f32[4,32,256]{2,1,0:T(8,128)}, u32[]{:S(2)}) copy-start(f32[4,32,256]{2,1,0:T(8,128)} %param.23) | copy-start | bytes 393220
  91.1 0.9 copy-start.9
  91.9 0.8 copy-start.11
  92.6 0.8 copy-start.13
  92.6 0.8 copy-start.14
  92.6 0.8 copy-start.18
  93.4 0.8 copy-start.17
  94.8 1.7 %copy-start.12 = (f32[20,32,256]{2,1,0:T(8,128)S(1)}, f32[20,32,256]{2,1,0:T(8,128)}, u32[]{:S(2)}) copy-start(f32[20,32,256]{2,1,0:T(8,128)} %get-tuple-element.96) | copy-start | bytes 1966084
  95.1 0.8 copy-start.16
